TPU v7x, 512 devices: a whole 4x8x8 slice. The times are simulated.
512 devices in a mesh: ctx: 64 (over x, z, core), tp: 8 (over y).
Axes of the slice: x: 4, y: 8, z: 8, core: 2. Of those that a mesh axis runs over, the one named last changes fastest.
Arguments:
- hyena_q: bfloat16 [8192, 8192], P('ctx', 'tp'), may hold values from -36 to 36
- hyena_k: bfloat16 [8192, 8192], P('ctx', 'tp'), may hold values from -6 to 6
- hyena_v: bfloat16 [8192, 8192], P('ctx', 'tp'), may hold values from -6 to 6
- filter_rate: float32 [8192, 16], P('tp'), may hold values from 0 to 1, as said below
- filter_residue: float32 [8192, 16], P('tp'), may hold values from -0.12 to 0.12
- skip_gain: float32 [8192], P('tp'), may hold values from 0.5 to 1.5
Outputs:
- hyena_out: bfloat16 [8192, 8192], P('ctx', 'tp')
Inputs may be any that keep to these rules, and one draw needn't show every extreme that they name: `filter_rate`: every rate is positive and at most 0.05.
All inputs are finite; a program needn't handle non-finite values.
Results may differ from a plain program's by a relative error of at most 0.0057.
Values may be sent and summed in bfloat16 or wider, within the bound.
No kernel may reach another device: no remote copies, remote signals or barrier semaphores. Data moves between devices by JAX's collectives and lax.ppermute only.
A program may use at most 64 MiB of HBM per device.

v0:
```python
import functools

import jax
import jax.numpy as jnp
from jax import lax
from jax.experimental import pallas as pl
from jax.experimental.pallas import tpu as pltpu
from jax.sharding import PartitionSpec as P

ORDER = 16
LANES = 128
SUBS = 8


def vmem_call(kernel, out_shape, scratch=(), name=None):
    return pl.pallas_call(
        kernel,
        out_shape=out_shape,
        scratch_shapes=scratch,
        name=name,
        compiler_params=pltpu.CompilerParams(vmem_limit_bytes=48 * 1024 * 1024),
    )


def fill_product(k_ref, v_ref, u_ref):
    tokens, width = k_ref.shape
    groups = width // LANES
    for pair in range(tokens // 16):
        for g in range(groups):
            rows, cols = pl.ds(pair * 16, 16), pl.ds(g * LANES, LANES)
            k = k_ref[rows, cols].astype(jnp.float32)
            v = v_ref[rows, cols].astype(jnp.float32)
            p = (k * v).astype(jnp.bfloat16).astype(jnp.float32)
            u_ref[pl.ds((2 * pair * groups + g) * SUBS, SUBS), :] = p[:SUBS]
            u_ref[pl.ds(((2 * pair + 1) * groups + g) * SUBS, SUBS), :] = p[SUBS:]


def fill_modes(src_ref, dst_ref, fn):
    groups = src_ref.shape[0] // LANES
    for g in range(groups):
        part = src_ref[pl.ds(g * LANES, LANES), :].T
        dst_ref[pl.ds(g, ORDER, stride=groups), :] = fn(part)


def state_kernel(k_ref, v_ref, rate_ref, end_ref, u_ref, q_ref):
    fill_modes(rate_ref, q_ref, lambda r: jnp.exp(-r))
    fill_product(k_ref, v_ref, u_ref)
    blocks = k_ref.shape[0] // SUBS

    def step(tb, xs):
        for i in range(SUBS):
            u = u_ref[pl.ds(tb * 64 + i, SUBS, stride=SUBS), :]
            xs = tuple(
                q_ref[pl.ds(m * SUBS, SUBS), :] * xs[m] + u for m in range(ORDER)
            )
        return xs

    zero = jnp.zeros((SUBS, LANES), jnp.float32)
    xs = lax.fori_loop(0, blocks, step, (zero,) * ORDER)
    for m in range(ORDER):
        end_ref[pl.ds(m * SUBS, SUBS), :] = xs[m]


def local_kernel(k_ref, v_ref, rate_ref, res_ref, skip_ref, z_ref, e_ref, q8_ref, u_ref, q_ref, r_ref):
    fill_modes(rate_ref, q_ref, lambda r: jnp.exp(-r))
    fill_modes(res_ref, r_ref, lambda r: r)
    fill_product(k_ref, v_ref, u_ref)
    blocks = k_ref.shape[0] // SUBS
    for m in range(ORDER):
        rows = pl.ds(m * SUBS, SUBS)
        q = q_ref[rows, :]
        w = r_ref[rows, :] * q
        for i in range(SUBS):
            e_ref[pl.ds(m * 64 + i, SUBS, stride=SUBS), :] = w
            w = w * q
        q2 = q * q
        q4 = q2 * q2
        q8_ref[rows, :] = q4 * q4

    def step(tb, xs):
        for i in range(SUBS):
            u = u_ref[pl.ds(tb * 64 + i, SUBS, stride=SUBS), :]
            z = skip_ref[...] * u
            new = []
            for m in range(ORDER):
                rows = pl.ds(m * SUBS, SUBS)
                x = q_ref[rows, :] * xs[m] + u
                z = z + r_ref[rows, :] * x
                new.append(x)
            xs = tuple(new)
            z_ref[pl.ds(tb * 64 + i, SUBS, stride=SUBS), :] = z
        return xs

    zero = jnp.zeros((SUBS, LANES), jnp.float32)
    lax.fori_loop(0, blocks, step, (zero,) * ORDER)


def scan_kernel(rate_ref, end_ref, start_ref):
    rows = rate_ref.shape[0]
    decay = jnp.exp(-float(LANES) * rate_ref[...])
    x = jnp.zeros((rows, LANES), jnp.float32)
    blocks = end_ref.shape[0] // rows
    for b in range(blocks):
        start_ref[pl.ds(b * rows, rows), :] = x
        if b < blocks - 1:
            x = decay * x + end_ref[pl.ds(b * rows, rows), :]


def gate_kernel(q_ref, z_ref, e_ref, q8_ref, s_ref, gated_ref, sums_ref, sq_ref):
    tokens, width = q_ref.shape
    groups = width // LANES
    for g in range(groups):
        vs, decays = [], []
        for m in range(ORDER):
            row = pl.ds(m * groups + g, 1)
            s = jnp.broadcast_to(s_ref[row, :], (SUBS, LANES))
            vs.append(s * e_ref[pl.ds((m * groups + g) * SUBS, SUBS), :])
            decays.append(jnp.broadcast_to(q8_ref[row, :], (SUBS, LANES)))
        for pair in range(tokens // 16):
            parts = []
            for half in range(2):
                tb = 2 * pair + half
                parts.append(z_ref[pl.ds((tb * groups + g) * SUBS, SUBS), :] + functools.reduce(jnp.add, vs))
                vs = [v * d for v, d in zip(vs, decays)]
            rows, cols = pl.ds(pair * 16, 16), pl.ds(g * LANES, LANES)
            wide = q_ref[rows, cols].astype(jnp.float32) * jnp.concatenate(parts, axis=0)
            gated = wide.astype(jnp.bfloat16)
            gated_ref[rows, cols] = gated
            square = gated.astype(jnp.float32)
            square = square * square
            if g == 0:
                sq_ref[rows, :] = square
            else:
                sq_ref[rows, :] = sq_ref[rows, :] + square
    sums_ref[...] = lax.dot_general(
        jnp.ones((SUBS, LANES), jnp.float32),
        sq_ref[...],
        (((1,), (1,)), ((), ())),
        precision=lax.Precision.HIGHEST,
        preferred_element_type=jnp.float32,
    )


def norm_kernel(scale, sums_ref, gated_ref, out_ref):
    tokens, width = gated_ref.shape
    total = lax.dot_general(
        sums_ref[...],
        jnp.ones((SUBS, LANES), jnp.float32),
        (((0,), (0,)), ((), ())),
        precision=lax.Precision.HIGHEST,
        preferred_element_type=jnp.float32,
    )
    inv = 1.0 / jnp.sqrt(total * scale + 1e-06)
    for g in range(width // LANES):
        cols = pl.ds(g * LANES, LANES)
        out_ref[:, cols] = (gated_ref[:, cols].astype(jnp.float32) * inv).astype(jnp.bfloat16)


def per_device(hyena_q, hyena_k, hyena_v, filter_rate, filter_residue, skip_gain):
    n_ctx = lax.axis_size("ctx")
    n_tp = lax.axis_size("tp")
    tokens, width = hyena_q.shape
    groups = width // LANES
    f32 = jnp.float32
    state = jax.ShapeDtypeStruct((ORDER * groups, LANES), f32)
    table = jax.ShapeDtypeStruct((tokens * groups, LANES), f32)
    plane = pltpu.VMEM((tokens * groups, LANES), f32)
    small = pltpu.VMEM((ORDER * groups, LANES), f32)

    ends = vmem_call(state_kernel, state, (plane, small), "states")(hyena_k, hyena_v, filter_rate)
    rows = ORDER * groups // n_ctx
    gathered = lax.all_to_all(
        ends.reshape(n_ctx, rows, LANES), "ctx", split_axis=0, concat_axis=0, tiled=True
    )
    z, e, q8 = vmem_call(
        local_kernel, (table, jax.ShapeDtypeStruct((ORDER * groups * SUBS, LANES), f32), state),
        (plane, small, small), "local",
    )(hyena_k, hyena_v, filter_rate, filter_residue, skip_gain.reshape(groups, LANES))
    rates = filter_rate.T.reshape(ORDER * groups, LANES)
    my_rates = lax.dynamic_slice_in_dim(rates, lax.axis_index("ctx") * rows, rows, 0)
    starts = vmem_call(scan_kernel, state, (), "scan")(
        my_rates, gathered.reshape(ORDER * groups, LANES)
    )
    carried = lax.all_to_all(
        starts.reshape(n_ctx, rows, LANES), "ctx", split_axis=0, concat_axis=0, tiled=True
    )
    gated, sums = vmem_call(
        gate_kernel,
        (jax.ShapeDtypeStruct((tokens, width), jnp.bfloat16), jax.ShapeDtypeStruct((n_tp, tokens), f32)),
        (pltpu.VMEM((tokens, LANES), f32),), "gate",
    )(hyena_q, z, e, q8, carried.reshape(ORDER * groups, LANES))
    all_sums = lax.all_to_all(sums, "tp", split_axis=0, concat_axis=0, tiled=True)
    return vmem_call(
        functools.partial(norm_kernel, 1.0 / (n_tp * width)),
        jax.ShapeDtypeStruct((tokens, width), jnp.bfloat16), (), "norm",
    )(all_sums, gated)


def solution(mesh):
    in_specs = (
        P("ctx", "tp"),
        P("ctx", "tp"),
        P("ctx", "tp"),
        P("tp", None),
        P("tp", None),
        P("tp"),
    )
    return jax.shard_map(
        per_device, mesh=mesh, in_specs=in_specs, out_specs=P("ctx", "tp"), check_vma=False
    )
```

profile of v0, /device:TPU:1, one launch (start us, length us, event | category | flops | bytes accessed | tf_op | source)
XLA Modules:
  0.0 57.6 jit_solution(5994909044386091262)
XLA Ops:
  0.0 0.0 copy-start
  0.0 0.0 copy-start.1
  0.0 1.1 %copy.10.rate_ref = f32[1024,16]{1,0:T(8,128)S(1)} copy(f32[1024,16]{0,1:T(8,128)} %param.9) | data formatting | bytes 131072 | tf_op args[3]
  1.1 0.0 copy-done
  1.1 0.0 copy-done.1
  1.1 1.5 %states.1 = f32[128,128]{1,0:T(8,128)} custom-call(bf16[128,1024]{1,0:T(8,128)(2,1)S(1)} %copy-done, bf16[128,1024]{1,0:T(8,128)(2,1)S(1)} %copy-done.1, f32[1024,16]{1,0:T(8,128)S(1)} %copy.10.rate_ref), custom_call_target="tpu_custom_call" | custom-call | tf_op jit(solution)/shard_map/states/pallas_call | solution.py:170
  2.6 0.0 copy-start.4
  2.6 15.0 %all-to-all-start = ((f32[64,2,128]{2,1,0:T(2,128)}), f32[64,2,128]{2,1,0:T(2,128)S(1)}, u32[]{:S(2)}, u32[]{:S(2)}) async-start(f32[64,2,128]{2,1,0:T(2,128)} %bitcast.2), calls=%async_computation | async-start | bytes 131072 | tf_op jit(solution)/shard_map/all_to_all | solution.py:172
  17.6 0.0 copy-done.4
  17.6 9.7 %all-to-all-done = f32[64,2,128]{2,1,0:T(2,128)S(1)} async-done(((f32[64,2,128]{2,1,0:T(2,128)}), f32[64,2,128]{2,1,0:T(2,128)S(1)}, u32[]{:S(2)}, u32[]{:S(2)}) %all-to-all-start) | async-done | bytes 65568 | tf_op jit(solution)/shard_map/all_to_all | solution.py:172
  27.3 0.8 %scan.1 = f32[128,128]{1,0:T(8,128)} custom-call(f32[2,128]{1,0:T(2,128)S(1)} %constant_dynamic-slice_fusion.rate_ref, f32[128,128]{1,0:T(8,128)S(1)} %bitcast.11), custom_call_target="tpu_custom_call" | custom-call | tf_op jit(solution)/shard_map/scan/pallas_call | solution.py:181
  28.1 0.0 copy-start.5
  28.1 4.6 %all-to-all-start.1 = ((f32[64,2,128]{2,1,0:T(2,128)}), f32[64,2,128]{2,1,0:T(2,128)S(1)}, u32[]{:S(2)}, u32[]{:S(2)}) async-start(f32[64,2,128]{2,1,0:T(2,128)} %bitcast.4), calls=%async_computation.1 | async-start | bytes 131072 | tf_op jit(solution)/shard_map/all_to_all | solution.py:184
  32.7 0.0 copy-done.5
  32.7 0.0 copy-start.3
  32.7 0.2 copy.11.res_ref
  32.9 0.5 copy-done.3
  33.4 0.0 copy-start.2
  33.4 1.7 %local.1 = (f32[1024,128]{1,0:T(8,128)S(1)}, f32[1024,128]{1,0:T(8,128)S(1)}, f32[128,128]{1,0:T(8,128)S(1)}) custom-call(bf16[128,1024]{1,0:T(8,128)(2,1)S(1)} %copy-done, bf16[128,1024]{1,0:T(8,128)(2,1)S(1)} %copy-done.1, f32[1024,16]{1,0:T(8,128)S(1)} %copy.10.rate_ref, f32[1024,16]{1,0:T(8,128)S(1)} %copy.11.res_ref, f32[8,128]{1,0:T(8,128)S(1)} %bitcast.13), custom_call_target="tpu_custom_call" | custom-call | tf_op jit(solution)/shard_map/local/pallas_call | solution.py:175
  35.2 7.4 %all-to-all-done.1 = f32[64,2,128]{2,1,0:T(2,128)S(1)} async-done(((f32[64,2,128]{2,1,0:T(2,128)}), f32[64,2,128]{2,1,0:T(2,128)S(1)}, u32[]{:S(2)}, u32[]{:S(2)}) %all-to-all-start.1) | async-done | bytes 65568 | tf_op jit(solution)/shard_map/all_to_all | solution.py:184
  42.6 0.0 copy-done.2
  42.6 0.9 %gate.1 = (bf16[128,1024]{1,0:T(8,128)(2,1)S(1)}, f32[8,128]{1,0:T(8,128)S(1)}) custom-call(bf16[128,1024]{1,0:T(8,128)(2,1)S(1)} %copy-done.2, f32[1024,128]{1,0:T(8,128)S(1)} %get-tuple-element.10.z_ref, f32[1024,128]{1,0:T(8,128)S(1)} %get-tuple-element.11.e_ref, f32[128,128]{1,0:T(8,128)S(1)} %get-tuple-element.12.q8_ref, f32[128,128]{1,0:T(8,128)S(1)} %bitcast.10), custom_call_target="tpu_custom_call" | custom-call | tf_op jit(solution)/shard_map/gate/pallas_call | solution.py:187
  43.5 13.2 %all_to_all.21 = f32[8,1,128]{2,1,0:T(1,128)S(1)} all-to-all(f32[8,1,128]{2,1,0:T(1,128)S(1)} %bitcast.14), channel_id=1, replica_groups=mesh['ctx'=64,'tp'=8] {'tp'}, dimensions={0} | all-to-all | bytes 8192 | tf_op jit(solution)/shard_map/all_to_all | solution.py:192
  56.6 1.0 %norm.1 = bf16[128,1024]{1,0:T(8,128)(2,1)} custom-call(f32[8,128]{1,0:T(8,128)S(1)} %bitcast.12, bf16[128,1024]{1,0:T(8,128)(2,1)S(1)} %get-tuple-element.14.gated_ref), custom_call_target="tpu_custom_call" | custom-call | tf_op jit(solution)/shard_map/norm/pallas_call | solution.py:193
  (2 shorter events, 0.0 us)
Async XLA Ops:
  0.0 1.1 %copy-start = (bf16[128,1024]{1,0:T(8,128)(2,1)S(1)}, bf16[128,1024]{1,0:T(8,128)(2,1)}, u32[]{:S(2)}) copy-start(bf16[128,1024]{1,0:T(8,128)(2,1)} %k_ref.3) | copy-start | bytes 786436
  0.0 1.1 %copy-start.1 = (bf16[128,1024]{1,0:T(8,128)(2,1)S(1)}, bf16[128,1024]{1,0:T(8,128)(2,1)}, u32[]{:S(2)}) copy-start(bf16[128,1024]{1,0:T(8,128)(2,1)} %v_ref.3) | copy-start | bytes 786436
  2.6 15.0 %copy-start.4 = (f32[1024,16]{0,1:T(8,128)S(1)}, f32[1024,16]{0,1:T(8,128)}, u32[]{:S(2)}) copy-start(f32[1024,16]{0,1:T(8,128)} %param.9) | copy-start | bytes 196612
  2.6 24.8 %all-to-all-start = ((f32[64,2,128]{2,1,0:T(2,128)}), f32[64,2,128]{2,1,0:T(2,128)S(1)}, u32[]{:S(2)}, u32[]{:S(2)}) async-start(f32[64,2,128]{2,1,0:T(2,128)} %bitcast.2), calls=%async_computation | async-start | bytes 131072 | tf_op jit(solution)/shard_map/all_to_all | solution.py:172
  28.1 4.6 %copy-start.5 = (f32[1024,16]{0,1:T(8,128)S(1)}, f32[1024,16]{0,1:T(8,128)}, u32[]{:S(2)}) copy-start(f32[1024,16]{0,1:T(8,128)} %param.10) | copy-start | bytes 196612
  28.1 14.5 %all-to-all-start.1 = ((f32[64,2,128]{2,1,0:T(2,128)}), f32[64,2,128]{2,1,0:T(2,128)S(1)}, u32[]{:S(2)}, u32[]{:S(2)}) async-start(f32[64,2,128]{2,1,0:T(2,128)} %bitcast.4), calls=%async_computation.1 | async-start | bytes 131072 | tf_op jit(solution)/shard_map/all_to_all | solution.py:184
  32.7 0.7 %copy-start.3 = (f32[1024]{0:T(1024)S(1)}, f32[1024]{0:T(1024)}, u32[]{:S(2)}) copy-start(f32[1024]{0:T(1024)} %param.11) | copy-start | bytes 12292
  33.4 9.2 %copy-start.2 = (bf16[128,1024]{1,0:T(8,128)(2,1)S(1)}, bf16[128,1024]{1,0:T(8,128)(2,1)}, u32[]{:S(2)}) copy-start(bf16[128,1024]{1,0:T(8,128)(2,1)} %q_ref.1) | copy-start | bytes 786436
where the time goes:
time: 58 us; the launch traced here: 57.6 us
  starting transfers between devices  19.5 us (34%)
  waiting for transfers between devices  17.2 us (30%)
  blocking collectives  13.2 us (23%)
  Pallas kernels  5.85 us (10%)
  local copies, waits for them, and re-layouts  1.81 us (3%)
    all_to_all x1, starting transfers between devices, per_device(): lax.all_to_all(ends.reshape(n_ctx, rows, LANES), 'ctx', split_axis=0, con...  15 us
    all_to_all x1, blocking collectives, per_device(): lax.all_to_all(sums, 'tp', split_axis=0, concat_axis=0, tiled=True)  13.2 us
    all_to_all x1, waiting for transfers between devices, per_device(): lax.all_to_all(ends.reshape(n_ctx, rows, LANES), 'ctx', split_axis=0, con...  9.73 us
    all_to_all x1, waiting for transfers between devices, per_device(): lax.all_to_all(starts.reshape(n_ctx, rows, LANES), 'ctx', split_axis=0, c...  7.44 us
    all_to_all x1, starting transfers between devices, per_device(): lax.all_to_all(starts.reshape(n_ctx, rows, LANES), 'ctx', split_axis=0, c...  4.58 us
    unnamed x14, local copies, waits for them, and re-layouts  1.78 us
    pallas_call x1, Pallas kernels, per_device(): vmem_call(local_kernel, (table, jax.ShapeDtypeStruct((ORDER * groups * SU...  1.75 us
    pallas_call x1, Pallas kernels, per_device(): vmem_call(state_kernel, state, (plane, small), 'states')  1.46 us
  transfers between devices with their start and end apart: 2, of which 2 were waited for; matrix products, arithmetic and copies ran while one was open for 0% of the time, Pallas kernels for 3%

commit v1 on v0

v1 whole, which is shorter than its diff:
```python
import functools

import jax
import jax.numpy as jnp
from jax import lax
from jax.experimental import pallas as pl
from jax.experimental.pallas import tpu as pltpu
from jax.sharding import PartitionSpec as P

ORDER = 16
LANES = 128
SUBS = 8
CORES = 2
RINGS = 8
Z_TYPE = jnp.float32
X_TYPE = jnp.float32


def call(kernel, out_shape, scratch=(), name=None, ins=None, outs=None):
    specs = {}
    if ins is not None:
        specs["in_specs"] = [pl.BlockSpec(memory_space=space) for space in ins]
    if outs is not None:
        specs["out_specs"] = pl.BlockSpec(memory_space=outs)
    return pl.pallas_call(
        kernel,
        out_shape=out_shape,
        scratch_shapes=scratch,
        name=name,
        compiler_params=pltpu.CompilerParams(vmem_limit_bytes=48 * 1024 * 1024),
        **specs,
    )


def fill_modes(src_ref, dst_ref, fn):
    groups = src_ref.shape[1] // LANES
    for g in range(groups):
        dst_ref[pl.ds(g, ORDER, stride=groups), :] = fn(src_ref[:, pl.ds(g * LANES, LANES)])


def state_kernel(k_hbm, v_hbm, rate_hbm, end_ref, u_ref, rows_ref, k_ref, v_ref, rate_ref, q_ref, sems, rate_sem):
    tokens, width = k_ref.shape
    groups = width // LANES
    pairs = tokens // 16

    def fetch(pair):
        rows = pl.ds(pair * 16, 16)
        return (
            pltpu.make_async_copy(k_hbm.at[rows, :], k_ref.at[rows, :], sems.at[0, pair]),
            pltpu.make_async_copy(v_hbm.at[rows, :], v_ref.at[rows, :], sems.at[1, pair]),
        )

    rates = pltpu.make_async_copy(rate_hbm, rate_ref, rate_sem)
    rates.start()
    for pair in range(pairs):
        for copy in fetch(pair):
            copy.start()
    rates.wait()
    fill_modes(rate_ref, rows_ref, lambda r: r)
    fill_modes(rate_ref, q_ref, lambda r: jnp.exp(-r))
    qs = tuple(q_ref[pl.ds(m * groups, groups), :] for m in range(ORDER))
    xs = (jnp.zeros((SUBS, LANES), jnp.float32),) * ORDER
    for pair in range(pairs):
        for copy in fetch(pair):
            copy.wait()
        rows = pl.ds(pair * 16, 16)
        for g in range(groups):
            cols = pl.ds(g * LANES, LANES)
            p = k_ref[rows, cols].astype(jnp.float32) * v_ref[rows, cols].astype(jnp.float32)
            p = p.astype(jnp.bfloat16).astype(jnp.float32)
            u_ref[pl.ds((2 * pair * groups + g) * SUBS, SUBS), :] = p[:SUBS]
            u_ref[pl.ds(((2 * pair + 1) * groups + g) * SUBS, SUBS), :] = p[SUBS:]

        def step(tb, xs):
            for i in range(SUBS):
                u = u_ref[pl.ds(tb * groups * SUBS + i, groups, stride=SUBS), :]
                xs = tuple(q * x + u for q, x in zip(qs, xs))
            return xs

        xs = lax.fori_loop(2 * pair, 2 * pair + 2, step, xs)
    for m in range(ORDER):
        end_ref[pl.ds(m * groups, groups), :] = xs[m]


def local_kernel(u_ref, rate_ref, res_ref, skip_ref, z_ref, e_ref, q8_ref, q_ref, r_ref):
    q_ref[...] = jnp.exp(-rate_ref[...])
    fill_modes(res_ref, r_ref, lambda r: r)
    for m in range(ORDER):
        rows = pl.ds(m * SUBS, SUBS)
        q = q_ref[rows, :]
        w = r_ref[rows, :] * q
        for i in range(SUBS):
            e_ref[pl.ds(m * 64 + i, SUBS, stride=SUBS), :] = w
            w = w * q
        q2 = q * q
        q4 = q2 * q2
        q8_ref[rows, :] = q4 * q4

    def step(tb, xs):
        for i in range(SUBS):
            u = u_ref[pl.ds(tb * 64 + i, SUBS, stride=SUBS), :]
            z = skip_ref[...] * u
            new = []
            for m in range(ORDER):
                rows = pl.ds(m * SUBS, SUBS)
                x = q_ref[rows, :] * xs[m] + u
                z = z + r_ref[rows, :] * x
                new.append(x)
            xs = tuple(new)
            z_ref[pl.ds(tb * 64 + i, SUBS, stride=SUBS), :] = z
        return xs

    zero = jnp.zeros((SUBS, LANES), jnp.float32)
    lax.fori_loop(0, u_ref.shape[0] // 64, step, (zero,) * ORDER)


def decay_of(rate, positions):
    return jnp.exp(rate * -positions)


def half_rates(rate_ref):
    half = rate_ref.shape[0] // CORES
    core = lax.axis_index("ctx") % CORES
    return pl.ds(pl.multiple_of(core * half, SUBS), half)


def chip_kernel(rate_ref, ends_ref, total_ref):
    rows = half_rates(rate_ref)
    decay = decay_of(rate_ref[rows, :], float(LANES))
    total = (decay * ends_ref[0, rows, :] + ends_ref[1, rows, :]).astype(total_ref.dtype)
    for copy in range(total_ref.shape[0]):
        total_ref[copy] = total


def prefix(part, count, decay, place):
    run = jnp.zeros(decay.shape, jnp.float32)
    before = run
    for n in range(count):
        before = jnp.where(place == n, run, before)
        run = decay * run + part(n).astype(jnp.float32)
    return before, run


def ring_kernel(rate_ref, totals_ref, before_ref, wholes_ref):
    place = lax.axis_index("ctx") // CORES % RINGS
    decay = decay_of(rate_ref[half_rates(rate_ref), :], float(CORES * LANES))
    before, run = prefix(lambda n: totals_ref[n], RINGS, decay, place)
    before_ref[...] = before
    whole = run.astype(wholes_ref.dtype)
    for copy in range(wholes_ref.shape[0]):
        wholes_ref[copy] = whole


def start_kernel(rate_ref, wholes_ref, before_ref, ends_ref, start_ref):
    me = lax.axis_index("ctx")
    x, z = me // (CORES * RINGS), me // CORES % RINGS
    rows = half_rates(rate_ref)
    rate = rate_ref[rows, :]
    far, _ = prefix(
        lambda n: wholes_ref[n], wholes_ref.shape[0], decay_of(rate, float(RINGS * CORES * LANES)), x
    )
    first = decay_of(rate, float(CORES * LANES) * z.astype(jnp.float32)) * far + before_ref[...]
    start_ref[0] = first
    start_ref[1] = decay_of(rate, float(LANES)) * first + ends_ref[0, rows, :]


def gate_kernel(q_ref, z_ref, e_ref, q8_ref, starts_ref, gated_ref, sums_ref, sq_ref):
    core = lax.axis_index("ctx") % CORES
    n_rows = starts_ref.shape[2]
    tokens, width = q_ref.shape
    groups = width // LANES
    for g in range(groups):
        vs, decays = [], []
        for m in range(ORDER):
            at = m * groups + g
            row = pl.ds(at, 1)
            s = starts_ref[at // n_rows, core, pl.ds(at % n_rows, 1), :]
            s = jnp.broadcast_to(s, (SUBS, LANES))
            vs.append(s * e_ref[pl.ds((m * groups + g) * SUBS, SUBS), :])
            decays.append(jnp.broadcast_to(q8_ref[row, :], (SUBS, LANES)))
        for pair in range(tokens // 16):
            parts = []
            for half in range(2):
                tb = 2 * pair + half
                parts.append(z_ref[pl.ds((tb * groups + g) * SUBS, SUBS), :] + functools.reduce(jnp.add, vs))
                vs = [v * d for v, d in zip(vs, decays)]
            rows, cols = pl.ds(pair * 16, 16), pl.ds(g * LANES, LANES)
            wide = q_ref[rows, cols].astype(jnp.float32) * jnp.concatenate(parts, axis=0)
            gated = wide.astype(jnp.bfloat16)
            gated_ref[rows, cols] = gated
            square = gated.astype(jnp.float32)
            square = square * square
            if g == 0:
                sq_ref[rows, :] = square
            else:
                sq_ref[rows, :] = sq_ref[rows, :] + square
    sums_ref[...] = lax.dot_general(
        jnp.ones((SUBS, LANES), jnp.float32),
        sq_ref[...],
        (((1,), (1,)), ((), ())),
        precision=lax.Precision.HIGHEST,
        preferred_element_type=jnp.float32,
    )


def norm_kernel(scale, sums_ref, gated_ref, out_hbm, out_ref, sems):
    tokens, width = gated_ref.shape
    chunks = sems.shape[0]
    total = lax.dot_general(
        sums_ref[...],
        jnp.ones((sums_ref.shape[0], LANES), jnp.float32),
        (((0,), (0,)), ((), ())),
        precision=lax.Precision.HIGHEST,
        preferred_element_type=jnp.float32,
    )
    inv = 1.0 / jnp.sqrt(total * scale + 1e-06)
    copies = []
    for chunk in range(chunks):
        size = tokens // chunks
        rows = pl.ds(chunk * size, size)
        part = inv[chunk * size:(chunk + 1) * size]
        for g in range(width // LANES):
            cols = pl.ds(g * LANES, LANES)
            out_ref[rows, cols] = (gated_ref[rows, cols].astype(jnp.float32) * part).astype(jnp.bfloat16)
        copies.append(pltpu.make_async_copy(out_ref.at[rows, :], out_hbm.at[rows, :], sems.at[chunk]))
        copies[-1].start()
    for copy in copies:
        copy.wait()


def per_device(hyena_q, hyena_k, hyena_v, filter_rate, filter_residue, skip_gain):
    n_ctx = lax.axis_size("ctx")
    n_tp = lax.axis_size("tp")
    tokens, width = hyena_q.shape
    groups = width // LANES
    f32, bf16 = jnp.float32, jnp.bfloat16
    rows = ORDER * groups
    half = rows // CORES
    shape = jax.ShapeDtypeStruct
    state = shape((rows, LANES), f32)
    table = shape((tokens * groups, LANES), f32)
    small = pltpu.VMEM((rows, LANES), f32)
    tile = pltpu.VMEM((tokens, width), bf16)
    n_x = n_ctx // (CORES * RINGS)
    pairs = [[CORES * i + c for c in range(CORES)] for i in range(n_ctx // CORES)]
    along_z = [
        [(x * RINGS + z) * CORES + c for z in range(RINGS)] for x in range(n_x) for c in range(CORES)
    ]
    along_x = [[x * RINGS * CORES + r for x in range(n_x)] for r in range(RINGS * CORES)]

    def swap(array, places):
        return lax.all_to_all(
            array, "ctx", split_axis=0, concat_axis=0, tiled=True, axis_index_groups=places
        )

    rate = filter_rate.T
    ends, u, rate_rows = call(
        state_kernel, (state, table, state),
        (tile, tile, pltpu.VMEM((ORDER, width), f32), small,
         pltpu.SemaphoreType.DMA((2, tokens // 16)), pltpu.SemaphoreType.DMA),
        "states", (pl.ANY,) * 3,
    )(*(pltpu.with_memory_space_constraint(a, pltpu.HBM) for a in (hyena_k, hyena_v, rate)))
    ends = lax.all_gather(ends, "ctx", axis_index_groups=pairs)
    totals = call(chip_kernel, shape((RINGS, half, LANES), Z_TYPE), (), "chip")(rate_rows, ends)
    totals = swap(totals, along_z)
    before, wholes = call(
        ring_kernel, (shape((half, LANES), f32), shape((n_x, half, LANES), X_TYPE)), (), "ring",
    )(rate_rows, totals)
    wholes = swap(wholes, along_x)
    starts = call(start_kernel, shape((CORES, half, LANES), f32), (), "start")(rate_rows, wholes, before, ends)
    starts = lax.all_gather(starts, "ctx", axis_index_groups=pairs)
    z, e, q8 = call(
        local_kernel, (table, shape((rows * SUBS, LANES), f32), state), (small, small), "local",
    )(u, rate_rows, filter_residue.T, skip_gain.reshape(groups, LANES))
    gated, sums = call(
        gate_kernel,
        (shape((tokens, width), bf16), shape((n_tp, tokens), f32)),
        (pltpu.VMEM((tokens, LANES), f32),), "gate",
    )(hyena_q, z, e, q8, starts)
    all_sums = lax.all_to_all(sums, "tp", split_axis=0, concat_axis=0, tiled=True)
    return call(
        functools.partial(norm_kernel, 1.0 / (n_tp * width)),
        shape((tokens, width), bf16), (tile, pltpu.SemaphoreType.DMA((4,))), "norm",
        (pltpu.VMEM,) * 2, pltpu.HBM,
    )(all_sums, gated)


def solution(mesh):
    in_specs = (
        P("ctx", "tp"),
        P("ctx", "tp"),
        P("ctx", "tp"),
        P("tp", None),
        P("tp", None),
        P("tp"),
    )
    return jax.shard_map(
        per_device, mesh=mesh, in_specs=in_specs, out_specs=P("ctx", "tp"), check_vma=False
    )
```

time: 58 us -> 56.1 us (0.967)
  blocking collectives: 13.2 us -> 42 us
  starting transfers between devices: 19.5 us -> 4.14 us
  waiting for transfers between devices: 17.2 us -> 2.73 us
  local copies, waits for them, and re-layouts: 1.81 us -> 0.69 us
    all_to_all x0 -> x1, blocking collectives: none -> 15.6 us  [swap(): lax.all_to_all(array, 'ctx', split_axis=0, concat_axis=0, tiled=True, axi...]
    all_to_all x2 -> x1, starting transfers between devices: 19.5 us -> 4.14 us  [swap(): lax.all_to_all(array, 'ctx', split_axis=0, concat_axis=0, tiled=True, axi...]
    all_to_all x2 -> x1, waiting for transfers between devices: 17.2 us -> 2.73 us  [swap(): lax.all_to_all(array, 'ctx', split_axis=0, concat_axis=0, tiled=True, axi...]
    all_gather x0 -> x2, blocking collectives: none -> 13.2 us  [the longest x1 8.43 us: per_device(): ends = lax.all_gather(ends, 'ctx', axis_index_groups=pairs)]
    unnamed x14 -> x6, local copies, waits for them, and re-layouts: 1.78 us -> 0.69 us
    pallas_call x5 -> x7, Pallas kernels: 5.85 us -> 6.08 us  [the longest x1 2.07 us: per_device(): call(state_kernel, (state, table, state), (tile, tile, pltpu.VMEM((ORDER,...]
  transfers between devices with their start and end apart: 2 -> 1, of which waited for: 2 -> 1; matrix products, arithmetic and copies ran while one was open for 0% -> 0% of each run, Pallas kernels for 3% -> 3%
where the time goes in v1:
time: 56.1 us; the launch traced here: 55.7 us
  blocking collectives  42 us (75%)
  Pallas kernels  6.08 us (11%)
  starting transfers between devices  4.14 us (7%)
  waiting for transfers between devices  2.73 us (5%)
  local copies, waits for them, and re-layouts  0.69 us (1%)
    all_to_all x1, blocking collectives, swap(): lax.all_to_all(array, 'ctx', split_axis=0, concat_axis=0, tiled=True, axi...  15.6 us
    all_to_all x1, blocking collectives, per_device(): lax.all_to_all(sums, 'tp', split_axis=0, concat_axis=0, tiled=True)  13.2 us
    all_gather x1, blocking collectives, per_device(): ends = lax.all_gather(ends, 'ctx', axis_index_groups=pairs)  8.43 us
    all_gather x1, blocking collectives, per_device(): starts = lax.all_gather(starts, 'ctx', axis_index_groups=pairs)  4.78 us
    all_to_all x1, starting transfers between devices, swap(): lax.all_to_all(array, 'ctx', split_axis=0, concat_axis=0, tiled=True, axi...  4.14 us
    all_to_all x1, waiting for transfers between devices, swap(): lax.all_to_all(array, 'ctx', split_axis=0, concat_axis=0, tiled=True, axi...  2.73 us
    pallas_call x1, Pallas kernels, per_device(): call(state_kernel, (state, table, state), (tile, tile, pltpu.VMEM((ORDER,...  2.07 us
    pallas_call x1, Pallas kernels, per_device(): call(local_kernel, (table, shape((rows * SUBS, LANES), f32), state), (sma...  1.4 us
  transfers between devices with their start and end apart: 1, of which 1 were waited for; matrix products, arithmetic and copies ran while one was open for 0% of the time, Pallas kernels for 3%

profile of v1, /device:TPU:1, one launch (start us, length us, event | category | flops | bytes accessed | tf_op | source)
XLA Modules:
  0.0 55.7 jit_solution(16682865839089120192)
XLA Ops:
  0.0 2.1 %states.1 = (f32[128,128]{1,0:T(8,128)S(1)}, f32[1024,128]{1,0:T(8,128)S(1)}, f32[128,128]{1,0:T(8,128)S(1)}) custom-call(bf16[128,1024]{1,0:T(8,128)(2,1)} %k_hbm.1, bf16[128,1024]{1,0:T(8,128)(2,1)} %v_hbm.1, f32[16,1024]{1,0:T(8,128)} %bitcast.16), custom_call_target="tpu_custom_call" | custom-call | tf_op jit(solution)/shard_map/states/pallas_call | solution.py:257
  2.1 8.4 %all-gather = f32[256,128]{1,0:T(8,128)S(1)} all-gather(f32[128,128]{1,0:T(8,128)S(1)} %get-tuple-element.20), channel_id=2, replica_groups={{0,8},{16,24},{32,40},{48,56},{64,72},{80,88},{96,104},{112,120},{128,1..., dimensions={0}, use_global_device_ids=true | all-gather | bytes 196608 | tf_op jit(solution)/shard_map/all_gather | solution.py:263
  10.5 15.6 %all_to_all.21.totals_ref = f32[8,64,128]{2,1,0:T(8,128)S(1)} all-to-all(f32[8,64,128]{2,1,0:T(8,128)S(1)} %chip.1), channel_id=1, replica_groups={{0,16,32,48,64,80,96,112},{8,24,40,56,72,88,104,120},{128,144,160,176,1..., dimensions={0} | all-to-all | bytes 524288 | tf_op jit(solution)/shard_map/all_to_all | solution.py:252
  26.2 0.7 %ring.1 = (f32[64,128]{1,0:T(8,128)S(1)}, f32[4,64,128]{2,1,0:T(8,128)}) custom-call(f32[128,128]{1,0:T(8,128)S(1)} %get-tuple-element.16.rate_ref, f32[8,64,128]{2,1,0:T(8,128)S(1)} %all_to_all.21.totals_ref), custom_call_target="tpu_custom_call" | custom-call | tf_op jit(solution)/shard_map/ring/pallas_call | solution.py:266
  26.8 0.0 copy-start.1
  26.9 4.1 %all-to-all-start.1 = ((f32[4,64,128]{2,1,0:T(8,128)}), f32[4,64,128]{2,1,0:T(8,128)S(1)}, u32[]{:S(2)}, u32[]{:S(2)}) async-start(f32[4,64,128]{2,1,0:T(8,128)} %get-tuple-element.21), calls=%async_computation.1 | async-start | bytes 262144 | tf_op jit(solution)/shard_map/all_to_all | solution.py:252
  31.0 0.0 copy-start.2
  31.0 0.0 copy-done.1
  31.0 0.7 %copy-done.2 = f32[1024]{0:T(1024)S(1)} copy-done((f32[1024]{0:T(1024)S(1)}, f32[1024]{0:T(1024)}, u32[]{:S(2)}) %copy-start.2) | copy-done | bytes 4120
  31.7 1.4 %local.1 = (f32[1024,128]{1,0:T(8,128)S(1)}, f32[1024,128]{1,0:T(8,128)S(1)}, f32[128,128]{1,0:T(8,128)S(1)}) custom-call(f32[1024,128]{1,0:T(8,128)S(1)} %get-tuple-element.15.u_ref, f32[128,128]{1,0:T(8,128)S(1)} %get-tuple-element.16.rate_ref, f32[16,1024]{1,0:T(8,128)S(1)} %bitcast.12, f32[8,128]{1,0:T(8,128)S(1)} %bitcast.14), custom_call_target="tpu_custom_call" | custom-call | tf_op jit(solution)/shard_map/local/pallas_call | solution.py:272
  33.1 2.7 %all-to-all-done.1.wholes_ref = f32[4,64,128]{2,1,0:T(8,128)S(1)} async-done(((f32[4,64,128]{2,1,0:T(8,128)}), f32[4,64,128]{2,1,0:T(8,128)S(1)}, u32[]{:S(2)}, u32[]{:S(2)}) %all-to-all-start.1) | async-done | bytes 131104 | tf_op jit(solution)/shard_map/all_to_all | solution.py:252
  35.8 0.0 copy-start
  35.9 4.8 %all-gather.1 = f32[4,64,128]{2,1,0:T(8,128)S(1)} all-gather(f32[2,64,128]{2,1,0:T(8,128)S(1)} %start.1), channel_id=3, replica_groups={{0,8},{16,24},{32,40},{48,56},{64,72},{80,88},{96,104},{112,120},{128,1..., dimensions={0}, use_global_device_ids=true | all-gather | bytes 196608 | tf_op jit(solution)/shard_map/all_gather | solution.py:271
  40.6 0.0 copy-done
  40.6 0.9 %gate.1 = (bf16[128,1024]{1,0:T(8,128)(2,1)S(1)}, f32[8,128]{1,0:T(8,128)S(1)}) custom-call(bf16[128,1024]{1,0:T(8,128)(2,1)S(1)} %copy-done, f32[1024,128]{1,0:T(8,128)S(1)} %get-tuple-element.17.z_ref, f32[1024,128]{1,0:T(8,128)S(1)} %get-tuple-element.18.e_ref, f32[128,128]{1,0:T(8,128)S(1)} %get-tuple-element.19.q8_ref, f32[2,2,64,128]{3,2,1,0:T(8,128)S(1)} %bitcast.11), custom_call_target="tpu_custom_call" | custom-call | tf_op jit(solution)/shard_map/gate/pallas_call | solution.py:275
  41.5 13.2 %all_to_all.22 = f32[8,1,128]{2,1,0:T(1,128)S(1)} all-to-all(f32[8,1,128]{2,1,0:T(1,128)S(1)} %bitcast.15), channel_id=1, replica_groups=mesh['ctx'=64,'tp'=8] {'tp'}, dimensions={0} | all-to-all | bytes 8192 | tf_op jit(solution)/shard_map/all_to_all | solution.py:280
  54.7 1.0 %norm.1 = bf16[128,1024]{1,0:T(8,128)(2,1)} custom-call(f32[8,128]{1,0:T(8,128)S(1)} %bitcast.13, bf16[128,1024]{1,0:T(8,128)(2,1)S(1)} %get-tuple-element.24.gated_ref), custom_call_target="tpu_custom_call" | custom-call | tf_op jit(solution)/shard_map/norm/pallas_call | solution.py:281
  (2 shorter events, 0.1 us)
Async XLA Ops:
  26.8 4.2 %copy-start.1 = (f32[1024,16]{0,1:T(8,128)S(1)}, f32[1024,16]{0,1:T(8,128)}, u32[]{:S(2)}) copy-start(f32[1024,16]{0,1:T(8,128)} %param.10) | copy-start | bytes 196612
  26.9 9.0 %all-to-all-start.1 = ((f32[4,64,128]{2,1,0:T(8,128)}), f32[4,64,128]{2,1,0:T(8,128)S(1)}, u32[]{:S(2)}, u32[]{:S(2)}) async-start(f32[4,64,128]{2,1,0:T(8,128)} %get-tuple-element.21), calls=%async_computation.1 | async-start | bytes 262144 | tf_op jit(solution)/shard_map/all_to_all | solution.py:252
  31.0 0.7 %copy-start.2 = (f32[1024]{0:T(1024)S(1)}, f32[1024]{0:T(1024)}, u32[]{:S(2)}) copy-start(f32[1024]{0:T(1024)} %param.11) | copy-start | bytes 12292
  35.8 4.8 %copy-start = (bf16[128,1024]{1,0:T(8,128)(2,1)S(1)}, bf16[128,1024]{1,0:T(8,128)(2,1)}, u32[]{:S(2)}) copy-start(bf16[128,1024]{1,0:T(8,128)(2,1)} %q_ref.1) | copy-start | bytes 786436

commit v2 on v1

--- a/solution.py
+++ b/solution.py
@@ -12,7 +12,8 @@
 SUBS = 8
 CORES = 2
 RINGS = 8
-Z_TYPE = jnp.float32
+CHUNKS = 4
+Z_TYPE = jnp.bfloat16
 X_TYPE = jnp.float32
 
 
@@ -38,80 +39,79 @@
         dst_ref[pl.ds(g, ORDER, stride=groups), :] = fn(src_ref[:, pl.ds(g * LANES, LANES)])
 
 
-def state_kernel(k_hbm, v_hbm, rate_hbm, end_ref, u_ref, rows_ref, k_ref, v_ref, rate_ref, q_ref, sems, rate_sem):
+def state_kernel(
+    k_hbm, v_hbm, rate_hbm, res_hbm, skip_hbm, end_ref, z_ref, e_ref, q8_ref, rate_rows_ref,
+    k_ref, v_ref, rate_ref, res_ref, skip_ref, u_ref, q_ref, r_ref, sems, mode_sems,
+):
     tokens, width = k_ref.shape
     groups = width // LANES
-    pairs = tokens // 16
-
-    def fetch(pair):
-        rows = pl.ds(pair * 16, 16)
+    chunks = sems.shape[1]
+    size = tokens // chunks
+
+    def fetch(chunk):
+        rows = pl.ds(chunk * size, size)
         return (
-            pltpu.make_async_copy(k_hbm.at[rows, :], k_ref.at[rows, :], sems.at[0, pair]),
-            pltpu.make_async_copy(v_hbm.at[rows, :], v_ref.at[rows, :], sems.at[1, pair]),
+            pltpu.make_async_copy(k_hbm.at[rows, :], k_ref.at[rows, :], sems.at[0, chunk]),
+            pltpu.make_async_copy(v_hbm.at[rows, :], v_ref.at[rows, :], sems.at[1, chunk]),
         )
 
-    rates = pltpu.make_async_copy(rate_hbm, rate_ref, rate_sem)
-    rates.start()
-    for pair in range(pairs):
-        for copy in fetch(pair):
+    modes = (
+        pltpu.make_async_copy(rate_hbm, rate_ref, mode_sems.at[0]),
+        pltpu.make_async_copy(res_hbm, res_ref, mode_sems.at[1]),
+        pltpu.make_async_copy(skip_hbm, skip_ref, mode_sems.at[2]),
+    )
+    for copy in modes:
+        copy.start()
+    for chunk in range(chunks):
+        for copy in fetch(chunk):
             copy.start()
-    rates.wait()
-    fill_modes(rate_ref, rows_ref, lambda r: r)
-    fill_modes(rate_ref, q_ref, lambda r: jnp.exp(-r))
-    qs = tuple(q_ref[pl.ds(m * groups, groups), :] for m in range(ORDER))
-    xs = (jnp.zeros((SUBS, LANES), jnp.float32),) * ORDER
-    for pair in range(pairs):
-        for copy in fetch(pair):
-            copy.wait()
-        rows = pl.ds(pair * 16, 16)
-        for g in range(groups):
-            cols = pl.ds(g * LANES, LANES)
-            p = k_ref[rows, cols].astype(jnp.float32) * v_ref[rows, cols].astype(jnp.float32)
-            p = p.astype(jnp.bfloat16).astype(jnp.float32)
-            u_ref[pl.ds((2 * pair * groups + g) * SUBS, SUBS), :] = p[:SUBS]
-            u_ref[pl.ds(((2 * pair + 1) * groups + g) * SUBS, SUBS), :] = p[SUBS:]
-
-        def step(tb, xs):
-            for i in range(SUBS):
-                u = u_ref[pl.ds(tb * groups * SUBS + i, groups, stride=SUBS), :]
-                xs = tuple(q * x + u for q, x in zip(qs, xs))
-            return xs
-
-        xs = lax.fori_loop(2 * pair, 2 * pair + 2, step, xs)
+    for copy in modes:
+        copy.wait()
+    fill_modes(rate_ref, rate_rows_ref, lambda r: r)
+    fill_modes(res_ref, r_ref, lambda r: r)
+    q_ref[...] = jnp.exp(-rate_rows_ref[...])
     for m in range(ORDER):
-        end_ref[pl.ds(m * groups, groups), :] = xs[m]
-
-
-def local_kernel(u_ref, rate_ref, res_ref, skip_ref, z_ref, e_ref, q8_ref, q_ref, r_ref):
-    q_ref[...] = jnp.exp(-rate_ref[...])
-    fill_modes(res_ref, r_ref, lambda r: r)
-    for m in range(ORDER):
-        rows = pl.ds(m * SUBS, SUBS)
+        rows = pl.ds(m * groups, groups)
         q = q_ref[rows, :]
         w = r_ref[rows, :] * q
         for i in range(SUBS):
-            e_ref[pl.ds(m * 64 + i, SUBS, stride=SUBS), :] = w
+            e_ref[pl.ds(m * groups * SUBS + i, groups, stride=SUBS), :] = w
             w = w * q
         q2 = q * q
         q4 = q2 * q2
         q8_ref[rows, :] = q4 * q4
-
-    def step(tb, xs):
-        for i in range(SUBS):
-            u = u_ref[pl.ds(tb * 64 + i, SUBS, stride=SUBS), :]
-            z = skip_ref[...] * u
-            new = []
-            for m in range(ORDER):
-                rows = pl.ds(m * SUBS, SUBS)
-                x = q_ref[rows, :] * xs[m] + u
-                z = z + r_ref[rows, :] * x
-                new.append(x)
-            xs = tuple(new)
-            z_ref[pl.ds(tb * 64 + i, SUBS, stride=SUBS), :] = z
-        return xs
-
-    zero = jnp.zeros((SUBS, LANES), jnp.float32)
-    lax.fori_loop(0, u_ref.shape[0] // 64, step, (zero,) * ORDER)
+    xs = (jnp.zeros((SUBS, LANES), jnp.float32),) * ORDER
+    for chunk in range(chunks):
+        for copy in fetch(chunk):
+            copy.wait()
+        for pair in range(chunk * size // 16, (chunk + 1) * size // 16):
+            rows = pl.ds(pair * 16, 16)
+            for g in range(groups):
+                cols = pl.ds(g * LANES, LANES)
+                p = k_ref[rows, cols].astype(jnp.float32) * v_ref[rows, cols].astype(jnp.float32)
+                p = p.astype(jnp.bfloat16).astype(jnp.float32)
+                u_ref[pl.ds((2 * pair * groups + g) * SUBS, SUBS), :] = p[:SUBS]
+                u_ref[pl.ds(((2 * pair + 1) * groups + g) * SUBS, SUBS), :] = p[SUBS:]
+
+        def step(tb, xs):
+            for i in range(SUBS):
+                at = pl.ds(tb * groups * SUBS + i, groups, stride=SUBS)
+                u = u_ref[at, :]
+                terms, new = [skip_ref[...] * u], []
+                for m in range(ORDER):
+                    rows = pl.ds(m * groups, groups)
+                    x = q_ref[rows, :] * xs[m] + u
+                    terms.append(r_ref[rows, :] * x)
+                    new.append(x)
+                xs = tuple(new)
+                while len(terms) > 1:
+                    terms = [functools.reduce(jnp.add, terms[n:n + 2]) for n in range(0, len(terms), 2)]
+                z_ref[at, :] = terms[0]
+            return xs
+
+        xs = lax.fori_loop(chunk * size // SUBS, (chunk + 1) * size // SUBS, step, xs)
+    for m in range(ORDER):
+        end_ref[pl.ds(m * groups, groups), :] = xs[m]
 
 
 def decay_of(rate, positions):
@@ -254,12 +254,17 @@
         )
 
     rate = filter_rate.T
-    ends, u, rate_rows = call(
-        state_kernel, (state, table, state),
-        (tile, tile, pltpu.VMEM((ORDER, width), f32), small,
-         pltpu.SemaphoreType.DMA((2, tokens // 16)), pltpu.SemaphoreType.DMA),
-        "states", (pl.ANY,) * 3,
-    )(*(pltpu.with_memory_space_constraint(a, pltpu.HBM) for a in (hyena_k, hyena_v, rate)))
+    weights = shape((rows * SUBS, LANES), f32)
+    modes = pltpu.VMEM((ORDER, width), f32)
+    ends, z, e, q8, rate_rows = call(
+        state_kernel, (state, table, weights, state, state),
+        (tile, tile, modes, modes, pltpu.VMEM((groups, LANES), f32), pltpu.VMEM(table.shape, f32), small, small,
+         pltpu.SemaphoreType.DMA((2, CHUNKS)), pltpu.SemaphoreType.DMA((3,))),
+        "states", (pltpu.HBM,) * 5,
+    )(*(
+        pltpu.with_memory_space_constraint(array, pltpu.HBM)
+        for array in (hyena_k, hyena_v, rate, filter_residue.T, skip_gain.reshape(groups, LANES))
+    ))
     ends = lax.all_gather(ends, "ctx", axis_index_groups=pairs)
     totals = call(chip_kernel, shape((RINGS, half, LANES), Z_TYPE), (), "chip")(rate_rows, ends)
     totals = swap(totals, along_z)
@@ -269,9 +274,6 @@
     wholes = swap(wholes, along_x)
     starts = call(start_kernel, shape((CORES, half, LANES), f32), (), "start")(rate_rows, wholes, before, ends)
     starts = lax.all_gather(starts, "ctx", axis_index_groups=pairs)
-    z, e, q8 = call(
-        local_kernel, (table, shape((rows * SUBS, LANES), f32), state), (small, small), "local",
-    )(u, rate_rows, filter_residue.T, skip_gain.reshape(groups, LANES))
     gated, sums = call(
         gate_kernel,
         (shape((tokens, width), bf16), shape((n_tp, tokens), f32)),

time: 56.1 us -> 52.9 us (0.943)
  blocking collectives: 42 us -> 47.8 us
  starting transfers between devices: 4.14 us -> 0 us
  waiting for transfers between devices: 2.73 us -> 0 us
  Pallas kernels: 6.08 us -> 4.73 us
  local copies, waits for them, and re-layouts: 0.69 us -> 0.01 us
    all_to_all x1 -> x2, blocking collectives: 15.6 us -> 21 us  [swap(): lax.all_to_all(array, 'ctx', split_axis=0, concat_axis=0, tiled=True, axi...]
    all_to_all x1 -> x0, starting transfers between devices: 4.14 us -> none  [swap(): lax.all_to_all(array, 'ctx', split_axis=0, concat_axis=0, tiled=True, axi...]
    all_to_all x1 -> x0, waiting for transfers between devices: 2.73 us -> none  [swap(): lax.all_to_all(array, 'ctx', split_axis=0, concat_axis=0, tiled=True, axi...]
    pallas_call x2 -> x1, Pallas kernels: 3.47 us -> 2.73 us  [per_device(): call(state_kernel, (state, table, weights, state, state), (tile, tile, mo...]
    unnamed x6 -> x2, local copies, waits for them, and re-layouts: 0.69 us -> 0.01 us
    pallas_call x1, Pallas kernels: 0.69 us -> 0.05 us  [per_device(): call(ring_kernel, (shape((half, LANES), f32), shape((n_x, half, LANES), X...]
  transfers between devices with their start and end apart: 1 -> 0, of which waited for: 1 -> 0; matrix products, arithmetic and copies ran while one was open for 0% -> 0% of each run, Pallas kernels for 3% -> 0%
where the time goes in v2:
time: 52.9 us; the launch traced here: 52.6 us
  blocking collectives  47.8 us (90%)
  Pallas kernels  4.73 us (9%)
    all_to_all x2, blocking collectives, swap(): lax.all_to_all(array, 'ctx', split_axis=0, concat_axis=0, tiled=True, axi...  21 us
    all_to_all x1, blocking collectives, per_device(): lax.all_to_all(sums, 'tp', split_axis=0, concat_axis=0, tiled=True)  13.2 us
    all_gather x1, blocking collectives, per_device(): ends = lax.all_gather(ends, 'ctx', axis_index_groups=pairs)  8.43 us
    all_gather x1, blocking collectives, per_device(): starts = lax.all_gather(starts, 'ctx', axis_index_groups=pairs)  5.21 us
    pallas_call x1, Pallas kernels, per_device(): call(state_kernel, (state, table, weights, state, state), (tile, tile, mo...  2.73 us

profile of v2, /device:TPU:1, one launch (start us, length us, event | category | flops | bytes accessed | tf_op | source)
XLA Modules:
  0.0 52.6 jit_solution(14654769551211777060)
XLA Ops:
  0.0 2.7 %states.1 = (f32[128,128]{1,0:T(8,128)S(1)}, f32[1024,128]{1,0:T(8,128)S(1)}, f32[1024,128]{1,0:T(8,128)S(1)}, f32[128,128]{1,0:T(8,128)S(1)}, f32[128,128]{1,0:T(8,128)S(1)}) custom-call(bf16[128,1024]{1,0:T(8,128)(2,1)} %k_hbm.1, bf16[128,1024]{1,0:T(8,128)(2,1)} %v_hbm.1, f32[16,1024]{1,0:T(8,128)} %bitcast.14, f32[16,1024]{1,0:T(8,128)} %bitcast.15, ...), custom_call_target="tpu_custom_call" | custom-call | tf_op jit(solution)/shard_map/states/pallas_call | solution.py:259
  2.7 8.4 %all-gather = f32[256,128]{1,0:T(8,128)S(1)} all-gather(f32[128,128]{1,0:T(8,128)S(1)} %get-tuple-element.18), channel_id=2, replica_groups={{0,8},{16,24},{32,40},{48,56},{64,72},{80,88},{96,104},{112,120},{128,1..., dimensions={0}, use_global_device_ids=true | all-gather | bytes 196608 | tf_op jit(solution)/shard_map/all_gather | solution.py:268
  11.2 12.4 %all_to_all.21.totals_ref = bf16[8,64,128]{2,1,0:T(8,128)(2,1)S(1)} all-to-all(bf16[8,64,128]{2,1,0:T(8,128)(2,1)S(1)} %chip.1), channel_id=1, replica_groups={{0,16,32,48,64,80,96,112},{8,24,40,56,72,88,104,120},{128,144,160,176,1..., dimensions={0} | all-to-all | bytes 262144 | tf_op jit(solution)/shard_map/all_to_all | solution.py:252
  23.6 0.1 ring.1
  23.6 8.6 %all_to_all.22.wholes_ref = f32[4,64,128]{2,1,0:T(8,128)S(1)} all-to-all(f32[4,64,128]{2,1,0:T(8,128)S(1)} %get-tuple-element.19), channel_id=1, replica_groups={{0,128,256,384},{8,136,264,392},{16,144,272,400},{24,152,280,408},{32,1..., dimensions={0} | all-to-all | bytes 262144 | tf_op jit(solution)/shard_map/all_to_all | solution.py:252
  32.3 0.0 copy-start
  32.3 5.2 %all-gather.1 = f32[4,64,128]{2,1,0:T(8,128)S(1)} all-gather(f32[2,64,128]{2,1,0:T(8,128)S(1)} %start.1), channel_id=3, replica_groups={{0,8},{16,24},{32,40},{48,56},{64,72},{80,88},{96,104},{112,120},{128,1..., dimensions={0}, use_global_device_ids=true | all-gather | bytes 196608 | tf_op jit(solution)/shard_map/all_gather | solution.py:276
  37.5 0.0 copy-done
  37.5 0.9 %gate.1 = (bf16[128,1024]{1,0:T(8,128)(2,1)S(1)}, f32[8,128]{1,0:T(8,128)S(1)}) custom-call(bf16[128,1024]{1,0:T(8,128)(2,1)S(1)} %copy-done, f32[1024,128]{1,0:T(8,128)S(1)} %get-tuple-element.14.z_ref, f32[1024,128]{1,0:T(8,128)S(1)} %get-tuple-element.15.e_ref, f32[128,128]{1,0:T(8,128)S(1)} %get-tuple-element.16.q8_ref, f32[2,2,64,128]{3,2,1,0:T(8,128)S(1)} %bitcast.11), custom_call_target="tpu_custom_call" | custom-call | tf_op jit(solution)/shard_map/gate/pallas_call | solution.py:277
  38.4 13.2 %all_to_all.23 = f32[8,1,128]{2,1,0:T(1,128)S(1)} all-to-all(f32[8,1,128]{2,1,0:T(1,128)S(1)} %bitcast.13), channel_id=1, replica_groups=mesh['ctx'=64,'tp'=8] {'tp'}, dimensions={0} | all-to-all | bytes 8192 | tf_op jit(solution)/shard_map/all_to_all | solution.py:282
  51.6 1.0 %norm.1 = bf16[128,1024]{1,0:T(8,128)(2,1)} custom-call(f32[8,128]{1,0:T(8,128)S(1)} %bitcast.12, bf16[128,1024]{1,0:T(8,128)(2,1)S(1)} %get-tuple-element.22.gated_ref), custom_call_target="tpu_custom_call" | custom-call | tf_op jit(solution)/shard_map/norm/pallas_call | solution.py:283
  (2 shorter events, 0.1 us)
Async XLA Ops:
  32.3 5.3 %copy-start = (bf16[128,1024]{1,0:T(8,128)(2,1)S(1)}, bf16[128,1024]{1,0:T(8,128)(2,1)}, u32[]{:S(2)}) copy-start(bf16[128,1024]{1,0:T(8,128)(2,1)} %q_ref.1) | copy-start | bytes 786436

commit v3 on v2

--- a/solution.py
+++ b/solution.py
@@ -12,9 +12,9 @@
 SUBS = 8
 CORES = 2
 RINGS = 8
-CHUNKS = 4
+CHUNKS = 2
 Z_TYPE = jnp.bfloat16
-X_TYPE = jnp.float32
+X_TYPE = jnp.bfloat16
 
 
 def call(kernel, out_shape, scratch=(), name=None, ins=None, outs=None):
@@ -80,6 +80,8 @@
         q2 = q * q
         q4 = q2 * q2
         q8_ref[rows, :] = q4 * q4
+    rs = tuple(r_ref[pl.ds(m * groups, groups), :] for m in range(ORDER))
+    qs = tuple(q_ref[pl.ds(m * groups, groups), :] for m in range(ORDER))
     xs = (jnp.zeros((SUBS, LANES), jnp.float32),) * ORDER
     for chunk in range(chunks):
         for copy in fetch(chunk):
@@ -100,8 +102,8 @@
                 terms, new = [skip_ref[...] * u], []
                 for m in range(ORDER):
                     rows = pl.ds(m * groups, groups)
-                    x = q_ref[rows, :] * xs[m] + u
-                    terms.append(r_ref[rows, :] * x)
+                    x = qs[m] * xs[m] + u
+                    terms.append(rs[m] * x)
                     new.append(x)
                 xs = tuple(new)
                 while len(terms) > 1:
@@ -141,41 +143,41 @@
     return before, run
 
 
-def ring_kernel(rate_ref, totals_ref, before_ref, wholes_ref):
-    place = lax.axis_index("ctx") // CORES % RINGS
+def ring_kernel(rate_ref, totals_ref, wholes_ref):
+    me = lax.axis_index("ctx")
     decay = decay_of(rate_ref[half_rates(rate_ref), :], float(CORES * LANES))
-    before, run = prefix(lambda n: totals_ref[n], RINGS, decay, place)
-    before_ref[...] = before
-    whole = run.astype(wholes_ref.dtype)
-    for copy in range(wholes_ref.shape[0]):
-        wholes_ref[copy] = whole
-
-
-def start_kernel(rate_ref, wholes_ref, before_ref, ends_ref, start_ref):
+    before, run = prefix(lambda n: totals_ref[n], RINGS, decay, me // CORES % RINGS)
+    x = me // (CORES * RINGS)
+    for n in range(wholes_ref.shape[0]):
+        wholes_ref[n] = jnp.where(x == n // CORES, before, run).astype(wholes_ref.dtype)
+
+
+def block_start(rate_ref, wholes_ref, ends_ref, s_ref):
     me = lax.axis_index("ctx")
-    x, z = me // (CORES * RINGS), me // CORES % RINGS
-    rows = half_rates(rate_ref)
-    rate = rate_ref[rows, :]
-    far, _ = prefix(
-        lambda n: wholes_ref[n], wholes_ref.shape[0], decay_of(rate, float(RINGS * CORES * LANES)), x
-    )
-    first = decay_of(rate, float(CORES * LANES) * z.astype(jnp.float32)) * far + before_ref[...]
-    start_ref[0] = first
-    start_ref[1] = decay_of(rate, float(LANES)) * first + ends_ref[0, rows, :]
-
-
-def gate_kernel(q_ref, z_ref, e_ref, q8_ref, starts_ref, gated_ref, sums_ref, sq_ref):
-    core = lax.axis_index("ctx") % CORES
-    n_rows = starts_ref.shape[2]
+    x, z, core = me // (CORES * RINGS), me // CORES % RINGS, me % CORES
+    half = wholes_ref.shape[1]
+    for h in range(CORES):
+        rows = pl.ds(h * half, half)
+        rate = rate_ref[rows, :]
+        far, _ = prefix(
+            lambda n: wholes_ref[n * CORES + h], wholes_ref.shape[0] // CORES,
+            decay_of(rate, float(RINGS * CORES * LANES)), x,
+        )
+        near = wholes_ref[x * CORES + h].astype(jnp.float32)
+        first = decay_of(rate, float(CORES * LANES) * z.astype(jnp.float32)) * far + near
+        second = decay_of(rate, float(LANES)) * first + ends_ref[0, rows, :]
+        s_ref[rows, :] = jnp.where(core == 0, first, second)
+
+
+def gate_kernel(q_ref, z_ref, e_ref, q8_ref, rate_ref, wholes_ref, ends_ref, gated_ref, sums_ref, sq_ref, s_ref):
+    block_start(rate_ref, wholes_ref, ends_ref, s_ref)
     tokens, width = q_ref.shape
     groups = width // LANES
     for g in range(groups):
         vs, decays = [], []
         for m in range(ORDER):
-            at = m * groups + g
-            row = pl.ds(at, 1)
-            s = starts_ref[at // n_rows, core, pl.ds(at % n_rows, 1), :]
-            s = jnp.broadcast_to(s, (SUBS, LANES))
+            row = pl.ds(m * groups + g, 1)
+            s = jnp.broadcast_to(s_ref[row, :], (SUBS, LANES))
             vs.append(s * e_ref[pl.ds((m * groups + g) * SUBS, SUBS), :])
             decays.append(jnp.broadcast_to(q8_ref[row, :], (SUBS, LANES)))
         for pair in range(tokens // 16):
@@ -246,7 +248,9 @@
     along_z = [
         [(x * RINGS + z) * CORES + c for z in range(RINGS)] for x in range(n_x) for c in range(CORES)
     ]
-    along_x = [[x * RINGS * CORES + r for x in range(n_x)] for r in range(RINGS * CORES)]
+    along_x = [
+        [(x * RINGS + z) * CORES + c for x in range(n_x) for c in range(CORES)] for z in range(RINGS)
+    ]
 
     def swap(array, places):
         return lax.all_to_all(
@@ -268,17 +272,13 @@
     ends = lax.all_gather(ends, "ctx", axis_index_groups=pairs)
     totals = call(chip_kernel, shape((RINGS, half, LANES), Z_TYPE), (), "chip")(rate_rows, ends)
     totals = swap(totals, along_z)
-    before, wholes = call(
-        ring_kernel, (shape((half, LANES), f32), shape((n_x, half, LANES), X_TYPE)), (), "ring",
-    )(rate_rows, totals)
+    wholes = call(ring_kernel, shape((n_x * CORES, half, LANES), X_TYPE), (), "ring")(rate_rows, totals)
     wholes = swap(wholes, along_x)
-    starts = call(start_kernel, shape((CORES, half, LANES), f32), (), "start")(rate_rows, wholes, before, ends)
-    starts = lax.all_gather(starts, "ctx", axis_index_groups=pairs)
     gated, sums = call(
         gate_kernel,
         (shape((tokens, width), bf16), shape((n_tp, tokens), f32)),
-        (pltpu.VMEM((tokens, LANES), f32),), "gate",
-    )(hyena_q, z, e, q8, starts)
+        (pltpu.VMEM((tokens, LANES), f32), small), "gate",
+    )(hyena_q, z, e, q8, rate_rows, wholes, ends)
     all_sums = lax.all_to_all(sums, "tp", split_axis=0, concat_axis=0, tiled=True)
     return call(
         functools.partial(norm_kernel, 1.0 / (n_tp * width)),

time: 52.9 us -> 50.4 us (0.953)
  blocking collectives: 47.8 us -> 45.6 us
    all_gather x1 -> x0, blocking collectives: 5.21 us -> none  [per_device(): starts = lax.all_gather(starts, 'ctx', axis_index_groups=pairs)]
    all_to_all x2, blocking collectives: 21 us -> 24 us  [swap(): lax.all_to_all(array, 'ctx', split_axis=0, concat_axis=0, tiled=True, axi...]
where the time goes in v3:
time: 50.4 us; the launch traced here: 50.2 us
  blocking collectives  45.6 us (90%)
  Pallas kernels  4.57 us (9%)
    all_to_all x2, blocking collectives, swap(): lax.all_to_all(array, 'ctx', split_axis=0, concat_axis=0, tiled=True, axi...  24 us
    all_to_all x1, blocking collectives, per_device(): lax.all_to_all(sums, 'tp', split_axis=0, concat_axis=0, tiled=True)  13.2 us
    all_gather x1, blocking collectives, per_device(): ends = lax.all_gather(ends, 'ctx', axis_index_groups=pairs)  8.43 us
    pallas_call x1, Pallas kernels, per_device(): call(state_kernel, (state, table, weights, state, state), (tile, tile, mo...  2.56 us

profile of v3, /device:TPU:1, one launch (start us, length us, event | category | flops | bytes accessed | tf_op | source)
XLA Modules:
  0.0 50.2 jit_solution(15584916376716387059)
XLA Ops:
  0.0 2.6 %states.1 = (f32[128,128]{1,0:T(8,128)S(1)}, f32[1024,128]{1,0:T(8,128)S(1)}, f32[1024,128]{1,0:T(8,128)S(1)}, f32[128,128]{1,0:T(8,128)S(1)}, f32[128,128]{1,0:T(8,128)S(1)}) custom-call(bf16[128,1024]{1,0:T(8,128)(2,1)} %k_hbm.1, bf16[128,1024]{1,0:T(8,128)(2,1)} %v_hbm.1, f32[16,1024]{1,0:T(8,128)} %bitcast.12, f32[16,1024]{1,0:T(8,128)} %bitcast.13, ...), custom_call_target="tpu_custom_call" | custom-call | tf_op jit(solution)/shard_map/states/pallas_call | solution.py:263
  2.6 8.4 %all-gather = f32[256,128]{1,0:T(8,128)S(1)} all-gather(f32[128,128]{1,0:T(8,128)S(1)} %get-tuple-element.16), channel_id=2, replica_groups={{0,8},{16,24},{32,40},{48,56},{64,72},{80,88},{96,104},{112,120},{128,1..., dimensions={0}, use_global_device_ids=true | all-gather | bytes 196608 | tf_op jit(solution)/shard_map/all_gather | solution.py:272
  11.0 12.4 %all_to_all.21.totals_ref = bf16[8,64,128]{2,1,0:T(8,128)(2,1)S(1)} all-to-all(bf16[8,64,128]{2,1,0:T(8,128)(2,1)S(1)} %chip.1), channel_id=1, replica_groups={{0,16,32,48,64,80,96,112},{8,24,40,56,72,88,104,120},{128,144,160,176,1..., dimensions={0} | all-to-all | bytes 262144 | tf_op jit(solution)/shard_map/all_to_all | solution.py:256
  23.4 0.0 copy-start
  23.4 0.1 ring.1
  23.5 11.6 %all_to_all.22.wholes_ref = bf16[8,64,128]{2,1,0:T(8,128)(2,1)S(1)} all-to-all(bf16[8,64,128]{2,1,0:T(8,128)(2,1)S(1)} %ring.1), channel_id=1, replica_groups={{0,8,128,136,256,264,384,392},{16,24,144,152,272,280,400,408},{32,40,16..., dimensions={0} | all-to-all | bytes 262144 | tf_op jit(solution)/shard_map/all_to_all | solution.py:256
  35.1 0.0 copy-done
  35.1 0.9 %gate.1 = (bf16[128,1024]{1,0:T(8,128)(2,1)S(1)}, f32[8,128]{1,0:T(8,128)S(1)}) custom-call(bf16[128,1024]{1,0:T(8,128)(2,1)S(1)} %copy-done, f32[1024,128]{1,0:T(8,128)S(1)} %get-tuple-element.12.z_ref, f32[1024,128]{1,0:T(8,128)S(1)} %get-tuple-element.13.e_ref, f32[128,128]{1,0:T(8,128)S(1)} %get-tuple-element.14.q8_ref, ...), custom_call_target="tpu_custom_call" | custom-call | tf_op jit(solution)/shard_map/gate/pallas_call | solution.py:277
  36.0 13.2 %all_to_all.23 = f32[8,1,128]{2,1,0:T(1,128)S(1)} all-to-all(f32[8,1,128]{2,1,0:T(1,128)S(1)} %bitcast.11), channel_id=1, replica_groups=mesh['ctx'=64,'tp'=8] {'tp'}, dimensions={0} | all-to-all | bytes 8192 | tf_op jit(solution)/shard_map/all_to_all | solution.py:282
  49.2 1.0 %norm.1 = bf16[128,1024]{1,0:T(8,128)(2,1)} custom-call(f32[8,128]{1,0:T(8,128)S(1)} %bitcast.10, bf16[128,1024]{1,0:T(8,128)(2,1)S(1)} %get-tuple-element.18.gated_ref), custom_call_target="tpu_custom_call" | custom-call | tf_op jit(solution)/shard_map/norm/pallas_call | solution.py:283
  (1 shorter events, 0.0 us)
Async XLA Ops:
  23.4 11.7 %copy-start = (bf16[128,1024]{1,0:T(8,128)(2,1)S(1)}, bf16[128,1024]{1,0:T(8,128)(2,1)}, u32[]{:S(2)}) copy-start(bf16[128,1024]{1,0:T(8,128)(2,1)} %q_ref.1) | copy-start | bytes 786436

commit v4 on v3

--- a/solution.py
+++ b/solution.py
@@ -12,6 +12,9 @@
 SUBS = 8
 CORES = 2
 RINGS = 8
+RING_ORDER = (5, 6, 7, 0, 1, 2, 3, 4)
+TP_ORDER = [4, 5, 6, 7, 0, 1, 2, 3]
+X_ORDER = ((2, 1), (0, 0), (0, 1), (1, 0), (1, 1), (2, 0), (3, 0), (3, 1))
 CHUNKS = 2
 Z_TYPE = jnp.bfloat16
 X_TYPE = jnp.bfloat16
@@ -146,10 +149,10 @@
 def ring_kernel(rate_ref, totals_ref, wholes_ref):
     me = lax.axis_index("ctx")
     decay = decay_of(rate_ref[half_rates(rate_ref), :], float(CORES * LANES))
-    before, run = prefix(lambda n: totals_ref[n], RINGS, decay, me // CORES % RINGS)
+    before, run = prefix(lambda n: totals_ref[RING_ORDER.index(n)], RINGS, decay, me // CORES % RINGS)
     x = me // (CORES * RINGS)
     for n in range(wholes_ref.shape[0]):
-        wholes_ref[n] = jnp.where(x == n // CORES, before, run).astype(wholes_ref.dtype)
+        wholes_ref[n] = jnp.where(x == X_ORDER[n][0], before, run).astype(wholes_ref.dtype)
 
 
 def block_start(rate_ref, wholes_ref, ends_ref, s_ref):
@@ -160,10 +163,13 @@
         rows = pl.ds(h * half, half)
         rate = rate_ref[rows, :]
         far, _ = prefix(
-            lambda n: wholes_ref[n * CORES + h], wholes_ref.shape[0] // CORES,
+            lambda n: wholes_ref[X_ORDER.index((n, h))], wholes_ref.shape[0] // CORES,
             decay_of(rate, float(RINGS * CORES * LANES)), x,
         )
-        near = wholes_ref[x * CORES + h].astype(jnp.float32)
+        near = wholes_ref[X_ORDER.index((0, h))]
+        for n in range(1, wholes_ref.shape[0] // CORES):
+            near = jnp.where(x == n, wholes_ref[X_ORDER.index((n, h))], near)
+        near = near.astype(jnp.float32)
         first = decay_of(rate, float(CORES * LANES) * z.astype(jnp.float32)) * far + near
         second = decay_of(rate, float(LANES)) * first + ends_ref[0, rows, :]
         s_ref[rows, :] = jnp.where(core == 0, first, second)
@@ -196,26 +202,16 @@
                 sq_ref[rows, :] = square
             else:
                 sq_ref[rows, :] = sq_ref[rows, :] + square
-    sums_ref[...] = lax.dot_general(
-        jnp.ones((SUBS, LANES), jnp.float32),
-        sq_ref[...],
-        (((1,), (1,)), ((), ())),
-        precision=lax.Precision.HIGHEST,
-        preferred_element_type=jnp.float32,
-    )
+    sums = jnp.sum(sq_ref[...].T, axis=0, keepdims=True)
+    sums_ref[...] = jnp.broadcast_to(sums, sums_ref.shape)
 
 
 def norm_kernel(scale, sums_ref, gated_ref, out_hbm, out_ref, sems):
     tokens, width = gated_ref.shape
     chunks = sems.shape[0]
-    total = lax.dot_general(
-        sums_ref[...],
-        jnp.ones((sums_ref.shape[0], LANES), jnp.float32),
-        (((0,), (0,)), ((), ())),
-        precision=lax.Precision.HIGHEST,
-        preferred_element_type=jnp.float32,
-    )
+    total = jnp.sum(sums_ref[...], axis=0, keepdims=True)
     inv = 1.0 / jnp.sqrt(total * scale + 1e-06)
+    inv = jnp.broadcast_to(inv, (LANES, tokens)).T
     copies = []
     for chunk in range(chunks):
         size = tokens // chunks
@@ -246,10 +242,10 @@
     n_x = n_ctx // (CORES * RINGS)
     pairs = [[CORES * i + c for c in range(CORES)] for i in range(n_ctx // CORES)]
     along_z = [
-        [(x * RINGS + z) * CORES + c for z in range(RINGS)] for x in range(n_x) for c in range(CORES)
+        [(x * RINGS + z) * CORES + c for z in RING_ORDER] for x in range(n_x) for c in range(CORES)
     ]
     along_x = [
-        [(x * RINGS + z) * CORES + c for x in range(n_x) for c in range(CORES)] for z in range(RINGS)
+        [(x * RINGS + z) * CORES + c for x, c in X_ORDER] for z in range(RINGS)
     ]
 
     def swap(array, places):
@@ -279,7 +275,9 @@
         (shape((tokens, width), bf16), shape((n_tp, tokens), f32)),
         (pltpu.VMEM((tokens, LANES), f32), small), "gate",
     )(hyena_q, z, e, q8, rate_rows, wholes, ends)
-    all_sums = lax.all_to_all(sums, "tp", split_axis=0, concat_axis=0, tiled=True)
+    all_sums = lax.all_to_all(
+        sums, "tp", split_axis=0, concat_axis=0, tiled=True, axis_index_groups=[TP_ORDER]
+    )
     return call(
         functools.partial(norm_kernel, 1.0 / (n_tp * width)),
         shape((tokens, width), bf16), (tile, pltpu.SemaphoreType.DMA((4,))), "norm",

time: 50.4 us -> 42.4 us (0.84)
  blocking collectives: 45.6 us -> 37.7 us
    all_to_all x2, blocking collectives: 24 us -> 19.9 us  [swap(): lax.all_to_all(array, 'ctx', split_axis=0, concat_axis=0, tiled=True, axi...]
    all_to_all x1, blocking collectives: 13.2 us -> 9.34 us  [per_device(): lax.all_to_all(sums, 'tp', split_axis=0, concat_axis=0, tiled=True, axis_...]
where the time goes in v4:
time: 42.4 us; the launch traced here: 42 us
  blocking collectives  37.7 us (89%)
  Pallas kernels  4.31 us (10%)
    all_to_all x2, blocking collectives, swap(): lax.all_to_all(array, 'ctx', split_axis=0, concat_axis=0, tiled=True, axi...  19.9 us
    all_to_all x1, blocking collectives, per_device(): lax.all_to_all(sums, 'tp', split_axis=0, concat_axis=0, tiled=True, axis_...  9.34 us
    all_gather x1, blocking collectives, per_device(): ends = lax.all_gather(ends, 'ctx', axis_index_groups=pairs)  8.43 us
    pallas_call x1, Pallas kernels, per_device(): call(state_kernel, (state, table, weights, state, state), (tile, tile, mo...  2.56 us

profile of v4, /device:TPU:1, one launch (start us, length us, event | category | flops | bytes accessed | tf_op | source)
XLA Modules:
  0.0 42.0 jit_solution(16382920531655353829)
XLA Ops:
  0.0 2.6 %states.1 = (f32[128,128]{1,0:T(8,128)S(1)}, f32[1024,128]{1,0:T(8,128)S(1)}, f32[1024,128]{1,0:T(8,128)S(1)}, f32[128,128]{1,0:T(8,128)S(1)}, f32[128,128]{1,0:T(8,128)S(1)}) custom-call(bf16[128,1024]{1,0:T(8,128)(2,1)} %k_hbm.1, bf16[128,1024]{1,0:T(8,128)(2,1)} %v_hbm.1, f32[16,1024]{1,0:T(8,128)} %bitcast.12, f32[16,1024]{1,0:T(8,128)} %bitcast.13, ...), custom_call_target="tpu_custom_call" | custom-call | tf_op jit(solution)/shard_map/states/pallas_call | solution.py:259
  2.6 8.4 %all-gather = f32[256,128]{1,0:T(8,128)S(1)} all-gather(f32[128,128]{1,0:T(8,128)S(1)} %get-tuple-element.16), channel_id=2, replica_groups={{0,8},{16,24},{32,40},{48,56},{64,72},{80,88},{96,104},{112,120},{128,1..., dimensions={0}, use_global_device_ids=true | all-gather | bytes 196608 | tf_op jit(solution)/shard_map/all_gather | solution.py:268
  11.0 10.6 %all_to_all.21.totals_ref = bf16[8,64,128]{2,1,0:T(8,128)(2,1)S(1)} all-to-all(bf16[8,64,128]{2,1,0:T(8,128)(2,1)S(1)} %chip.1), channel_id=1, replica_groups={{80,96,112,0,16,32,48,64},{88,104,120,8,24,40,56,72},{208,224,240,128,1..., dimensions={0} | all-to-all | bytes 262144 | tf_op jit(solution)/shard_map/all_to_all | solution.py:252
  21.7 0.0 copy-start
  21.7 0.1 ring.1
  21.7 9.3 %all_to_all.22.wholes_ref = bf16[8,64,128]{2,1,0:T(8,128)(2,1)S(1)} all-to-all(bf16[8,64,128]{2,1,0:T(8,128)(2,1)S(1)} %ring.1), channel_id=1, replica_groups={{264,0,8,128,136,256,384,392},{280,16,24,144,152,272,400,408},{296,32,4..., dimensions={0} | all-to-all | bytes 262144 | tf_op jit(solution)/shard_map/all_to_all | solution.py:252
  31.0 0.0 copy-done
  31.0 0.8 %gate.1 = (bf16[128,1024]{1,0:T(8,128)(2,1)S(1)}, f32[8,128]{1,0:T(8,128)S(1)}) custom-call(bf16[128,1024]{1,0:T(8,128)(2,1)S(1)} %copy-done, f32[1024,128]{1,0:T(8,128)S(1)} %get-tuple-element.12.z_ref, f32[1024,128]{1,0:T(8,128)S(1)} %get-tuple-element.13.e_ref, f32[128,128]{1,0:T(8,128)S(1)} %get-tuple-element.14.q8_ref, ...), custom_call_target="tpu_custom_call" | custom-call | tf_op jit(solution)/shard_map/gate/pallas_call | solution.py:273
  31.9 9.3 %all_to_all.23 = f32[8,1,128]{2,1,0:T(1,128)S(1)} all-to-all(f32[8,1,128]{2,1,0:T(1,128)S(1)} %bitcast.11), channel_id=1, replica_groups={{4,5,6,7,0,1,2,3},{12,13,14,15,8,9,10,11},{20,21,22,23,16,17,18,19},{28..., dimensions={0} | all-to-all | bytes 8192 | tf_op jit(solution)/shard_map/all_to_all | solution.py:278
  41.2 0.8 %norm.1 = bf16[128,1024]{1,0:T(8,128)(2,1)} custom-call(f32[8,128]{1,0:T(8,128)S(1)} %bitcast.10, bf16[128,1024]{1,0:T(8,128)(2,1)S(1)} %get-tuple-element.18.gated_ref), custom_call_target="tpu_custom_call" | custom-call | tf_op jit(solution)/shard_map/norm/pallas_call | solution.py:281
  (1 shorter events, 0.0 us)
Async XLA Ops:
  21.7 9.4 %copy-start = (bf16[128,1024]{1,0:T(8,128)(2,1)S(1)}, bf16[128,1024]{1,0:T(8,128)(2,1)}, u32[]{:S(2)}) copy-start(bf16[128,1024]{1,0:T(8,128)(2,1)} %q_ref.1) | copy-start | bytes 786436

commit v5 on v4

--- a/solution.py
+++ b/solution.py
@@ -12,7 +12,7 @@
 SUBS = 8
 CORES = 2
 RINGS = 8
-RING_ORDER = (5, 6, 7, 0, 1, 2, 3, 4)
+RING_ORDER = (6, 7, 0, 1, 2, 3, 4, 5)
 TP_ORDER = [4, 5, 6, 7, 0, 1, 2, 3]
 X_ORDER = ((2, 1), (0, 0), (0, 1), (1, 0), (1, 1), (2, 0), (3, 0), (3, 1))
 CHUNKS = 2
@@ -20,7 +20,7 @@
 X_TYPE = jnp.bfloat16
 
 
-def call(kernel, out_shape, scratch=(), name=None, ins=None, outs=None):
+def call(kernel, out_shape, scratch=(), name=None, ins=None, outs=None, aliases={}):
     specs = {}
     if ins is not None:
         specs["in_specs"] = [pl.BlockSpec(memory_space=space) for space in ins]
@@ -30,6 +30,7 @@
         kernel,
         out_shape=out_shape,
         scratch_shapes=scratch,
+        input_output_aliases=aliases,
         name=name,
         compiler_params=pltpu.CompilerParams(vmem_limit_bytes=48 * 1024 * 1024),
         **specs,
@@ -43,8 +44,8 @@
 
 
 def state_kernel(
-    k_hbm, v_hbm, rate_hbm, res_hbm, skip_hbm, end_ref, z_ref, e_ref, q8_ref, rate_rows_ref,
-    k_ref, v_ref, rate_ref, res_ref, skip_ref, u_ref, q_ref, r_ref, sems, mode_sems,
+    k_hbm, v_hbm, rate_hbm, res_hbm, skip_hbm, end_ref, z_ref, e_ref, q8_ref, rate_rows_ref, u_ref, r_ref, skip_ref,
+    k_ref, v_ref, rate_ref, res_ref, q_ref, sems, mode_sems,
 ):
     tokens, width = k_ref.shape
     groups = width // LANES
@@ -83,9 +84,6 @@
         q2 = q * q
         q4 = q2 * q2
         q8_ref[rows, :] = q4 * q4
-    rs = tuple(r_ref[pl.ds(m * groups, groups), :] for m in range(ORDER))
-    qs = tuple(q_ref[pl.ds(m * groups, groups), :] for m in range(ORDER))
-    xs = (jnp.zeros((SUBS, LANES), jnp.float32),) * ORDER
     for chunk in range(chunks):
         for copy in fetch(chunk):
             copy.wait()
@@ -97,26 +95,47 @@
                 p = p.astype(jnp.bfloat16).astype(jnp.float32)
                 u_ref[pl.ds((2 * pair * groups + g) * SUBS, SUBS), :] = p[:SUBS]
                 u_ref[pl.ds(((2 * pair + 1) * groups + g) * SUBS, SUBS), :] = p[SUBS:]
-
-        def step(tb, xs):
-            for i in range(SUBS):
-                at = pl.ds(tb * groups * SUBS + i, groups, stride=SUBS)
-                u = u_ref[at, :]
-                terms, new = [skip_ref[...] * u], []
-                for m in range(ORDER):
-                    rows = pl.ds(m * groups, groups)
-                    x = qs[m] * xs[m] + u
-                    terms.append(rs[m] * x)
-                    new.append(x)
-                xs = tuple(new)
+        blocks = (chunk * size // SUBS, (chunk + 1) * size // SUBS)
+
+        @pl.when(defers())
+        def _():
+            recur(*blocks, end_ref, u_ref, q_ref, None, None, None)
+
+        @pl.when(jnp.logical_not(defers()))
+        def _():
+            recur(*blocks, end_ref, u_ref, q_ref, r_ref, skip_ref, z_ref)
+
+
+def defers():
+    return lax.axis_index("ctx") // CORES % RINGS >= RINGS // 2
+
+
+def recur(first, last, x_ref, u_ref, q_ref, r_ref, skip_ref, z_ref):
+    groups = SUBS
+    rows = [pl.ds(m * groups, groups) for m in range(ORDER)]
+    qs = tuple(q_ref[at, :] for at in rows)
+    if z_ref is not None:
+        rs = tuple(r_ref[at, :] for at in rows)
+
+    def step(tb, xs):
+        for i in range(SUBS):
+            at = pl.ds(tb * groups * SUBS + i, groups, stride=SUBS)
+            u = u_ref[at, :]
+            xs = tuple(q * x + u for q, x in zip(qs, xs))
+            if z_ref is not None:
+                terms = [skip_ref[...] * u] + [r * x for r, x in zip(rs, xs)]
                 while len(terms) > 1:
                     terms = [functools.reduce(jnp.add, terms[n:n + 2]) for n in range(0, len(terms), 2)]
                 z_ref[at, :] = terms[0]
-            return xs
-
-        xs = lax.fori_loop(chunk * size // SUBS, (chunk + 1) * size // SUBS, step, xs)
-    for m in range(ORDER):
-        end_ref[pl.ds(m * groups, groups), :] = xs[m]
+        return xs
+
+    if first == 0:
+        xs = (jnp.zeros((groups, LANES), jnp.float32),) * ORDER
+    else:
+        xs = tuple(x_ref[at, :] for at in rows)
+    xs = lax.fori_loop(first, last, step, xs)
+    for at, x in zip(rows, xs):
+        x_ref[at, :] = x
 
 
 def decay_of(rate, positions):
@@ -146,13 +165,18 @@
     return before, run
 
 
-def ring_kernel(rate_ref, totals_ref, wholes_ref):
+def ring_kernel(rate_ref, totals_ref, u_ref, r_ref, skip_ref, z_in_ref, wholes_ref, z_ref, q_ref, x_ref):
     me = lax.axis_index("ctx")
     decay = decay_of(rate_ref[half_rates(rate_ref), :], float(CORES * LANES))
     before, run = prefix(lambda n: totals_ref[RING_ORDER.index(n)], RINGS, decay, me // CORES % RINGS)
     x = me // (CORES * RINGS)
     for n in range(wholes_ref.shape[0]):
         wholes_ref[n] = jnp.where(x == X_ORDER[n][0], before, run).astype(wholes_ref.dtype)
+
+    @pl.when(defers())
+    def _():
+        q_ref[...] = jnp.exp(-rate_ref[...])
+        recur(0, u_ref.shape[0] // (SUBS * SUBS), x_ref, u_ref, q_ref, r_ref, skip_ref, z_ref)
 
 
 def block_start(rate_ref, wholes_ref, ends_ref, s_ref):
@@ -256,9 +280,9 @@
     rate = filter_rate.T
     weights = shape((rows * SUBS, LANES), f32)
     modes = pltpu.VMEM((ORDER, width), f32)
-    ends, z, e, q8, rate_rows = call(
-        state_kernel, (state, table, weights, state, state),
-        (tile, tile, modes, modes, pltpu.VMEM((groups, LANES), f32), pltpu.VMEM(table.shape, f32), small, small,
+    ends, z, e, q8, rate_rows, u, residues, skip = call(
+        state_kernel, (state, table, weights, state, state, table, state, shape((groups, LANES), f32)),
+        (tile, tile, modes, modes, small,
          pltpu.SemaphoreType.DMA((2, CHUNKS)), pltpu.SemaphoreType.DMA((3,))),
         "states", (pltpu.HBM,) * 5,
     )(*(
@@ -268,7 +292,9 @@
     ends = lax.all_gather(ends, "ctx", axis_index_groups=pairs)
     totals = call(chip_kernel, shape((RINGS, half, LANES), Z_TYPE), (), "chip")(rate_rows, ends)
     totals = swap(totals, along_z)
-    wholes = call(ring_kernel, shape((n_x * CORES, half, LANES), X_TYPE), (), "ring")(rate_rows, totals)
+    wholes, z = call(
+        ring_kernel, (shape((n_x * CORES, half, LANES), X_TYPE), table), (small, small), "ring", aliases={5: 1},
+    )(rate_rows, totals, u, residues, skip, z)
     wholes = swap(wholes, along_x)
     gated, sums = call(
         gate_kernel,

time: 42.4 us -> 41.4 us (0.976)
  blocking collectives: 37.7 us -> 36.6 us
    all_to_all x2, blocking collectives: 19.9 us -> 18.9 us  [swap(): lax.all_to_all(array, 'ctx', split_axis=0, concat_axis=0, tiled=True, axi...]
where the time goes in v5:
time: 41.4 us; the launch traced here: 41 us
  blocking collectives  36.6 us (88%)
  Pallas kernels  4.36 us (11%)
    all_to_all x2, blocking collectives, swap(): lax.all_to_all(array, 'ctx', split_axis=0, concat_axis=0, tiled=True, axi...  18.9 us
    all_to_all x1, blocking collectives, per_device(): lax.all_to_all(sums, 'tp', split_axis=0, concat_axis=0, tiled=True, axis_...  9.34 us
    all_gather x1, blocking collectives, per_device(): ends = lax.all_gather(ends, 'ctx', axis_index_groups=pairs)  8.43 us
    pallas_call x1, Pallas kernels, per_device(): call(state_kernel, (state, table, weights, state, state, table, state, sh...  2.53 us
    pallas_call x1, Pallas kernels, per_device(): call(gate_kernel, (shape((tokens, width), bf16), shape((n_tp, tokens), f3...  0.92 us
    pallas_call x1, Pallas kernels, per_device(): call(functools.partial(norm_kernel, 1.0 / (n_tp * width)), shape((tokens,...  0.83 us

profile of v5, /device:TPU:1, one launch (start us, length us, event | category | flops | bytes accessed | tf_op | source)
XLA Modules:
  0.0 41.0 jit_solution(3698152986960572896)
XLA Ops:
  0.0 2.5 %states.1 = (f32[128,128]{1,0:T(8,128)S(1)}, f32[1024,128]{1,0:T(8,128)S(1)}, f32[1024,128]{1,0:T(8,128)S(1)}, f32[128,128]{1,0:T(8,128)S(1)}, f32[128,128]{1,0:...) custom-call(bf16[128,1024]{1,0:T(8,128)(2,1)} %k_hbm.1, ...), custom_call_target="tpu_custom_call" | custom-call | tf_op jit(solution)/shard_map/states/pallas_call | solution.py:283
  2.5 8.4 %all-gather = f32[256,128]{1,0:T(8,128)S(1)} all-gather(f32[128,128]{1,0:T(8,128)S(1)} %get-tuple-element.18), channel_id=2, replica_groups={{0,8},{16,24},{32,40},{48,56},{64,72},{80,88},{96,104},{112,120},{128,1..., dimensions={0}, use_global_device_ids=true | all-gather | bytes 196608 | tf_op jit(solution)/shard_map/all_gather | solution.py:292
  11.0 9.4 %all_to_all.21.totals_ref = bf16[8,64,128]{2,1,0:T(8,128)(2,1)S(1)} all-to-all(bf16[8,64,128]{2,1,0:T(8,128)(2,1)S(1)} %chip.1), channel_id=1, replica_groups={{96,112,0,16,32,48,64,80},{104,120,8,24,40,56,72,88},{224,240,128,144,1..., dimensions={0} | all-to-all | bytes 262144 | tf_op jit(solution)/shard_map/all_to_all | solution.py:276
  20.4 0.1 ring.1
  20.5 0.0 copy-start
  20.5 9.5 %all_to_all.22.wholes_ref = bf16[8,64,128]{2,1,0:T(8,128)(2,1)S(1)} all-to-all(bf16[8,64,128]{2,1,0:T(8,128)(2,1)S(1)} %get-tuple-element.26), channel_id=1, replica_groups={{264,0,8,128,136,256,384,392},{280,16,24,144,152,272,400,408},{296,32,4..., dimensions={0} | all-to-all | bytes 262144 | tf_op jit(solution)/shard_map/all_to_all | solution.py:276
  29.9 0.0 copy-done
  29.9 0.9 %gate.1 = (bf16[128,1024]{1,0:T(8,128)(2,1)S(1)}, f32[8,128]{1,0:T(8,128)S(1)}) custom-call(bf16[128,1024]{1,0:T(8,128)(2,1)S(1)} %copy-done, f32[1024,128]{1,0:T(8,128)S(1)} %get-tuple-element.23.z_ref, f32[1024,128]{1,0:T(8,128)S(1)} %get-tuple-element.24.e_ref, f32[128,128]{1,0:T(8,128)S(1)} %get-tuple-element.25.q8_ref, ...), custom_call_target="tpu_custom_call" | custom-call | tf_op jit(solution)/shard_map/gate/pallas_call | solution.py:299
  30.9 9.3 %all_to_all.23 = f32[8,1,128]{2,1,0:T(1,128)S(1)} all-to-all(f32[8,1,128]{2,1,0:T(1,128)S(1)} %bitcast.11), channel_id=1, replica_groups={{4,5,6,7,0,1,2,3},{12,13,14,15,8,9,10,11},{20,21,22,23,16,17,18,19},{28..., dimensions={0} | all-to-all | bytes 8192 | tf_op jit(solution)/shard_map/all_to_all | solution.py:304
  40.2 0.8 %norm.1 = bf16[128,1024]{1,0:T(8,128)(2,1)} custom-call(f32[8,128]{1,0:T(8,128)S(1)} %bitcast.10, bf16[128,1024]{1,0:T(8,128)(2,1)S(1)} %get-tuple-element.28.gated_ref), custom_call_target="tpu_custom_call" | custom-call | tf_op jit(solution)/shard_map/norm/pallas_call | solution.py:307
  (1 shorter events, 0.0 us)
Async XLA Ops:
  20.5 9.5 %copy-start = (bf16[128,1024]{1,0:T(8,128)(2,1)S(1)}, bf16[128,1024]{1,0:T(8,128)(2,1)}, u32[]{:S(2)}) copy-start(bf16[128,1024]{1,0:T(8,128)(2,1)} %q_ref.1) | copy-start | bytes 786436

commit v6 on v5

--- a/solution.py
+++ b/solution.py
@@ -43,6 +43,20 @@
         dst_ref[pl.ds(g, ORDER, stride=groups), :] = fn(src_ref[:, pl.ds(g * LANES, LANES)])
 
 
+def tables(q_ref, r_ref, e_ref, q8_ref):
+    groups = SUBS
+    for m in range(ORDER):
+        rows = pl.ds(m * groups, groups)
+        q = q_ref[rows, :]
+        w = r_ref[rows, :] * q
+        for i in range(SUBS):
+            e_ref[pl.ds(m * groups * SUBS + i, groups, stride=SUBS), :] = w
+            w = w * q
+        q2 = q * q
+        q4 = q2 * q2
+        q8_ref[rows, :] = q4 * q4
+
+
 def state_kernel(
     k_hbm, v_hbm, rate_hbm, res_hbm, skip_hbm, end_ref, z_ref, e_ref, q8_ref, rate_rows_ref, u_ref, r_ref, skip_ref,
     k_ref, v_ref, rate_ref, res_ref, q_ref, sems, mode_sems,
@@ -74,16 +88,10 @@
     fill_modes(rate_ref, rate_rows_ref, lambda r: r)
     fill_modes(res_ref, r_ref, lambda r: r)
     q_ref[...] = jnp.exp(-rate_rows_ref[...])
-    for m in range(ORDER):
-        rows = pl.ds(m * groups, groups)
-        q = q_ref[rows, :]
-        w = r_ref[rows, :] * q
-        for i in range(SUBS):
-            e_ref[pl.ds(m * groups * SUBS + i, groups, stride=SUBS), :] = w
-            w = w * q
-        q2 = q * q
-        q4 = q2 * q2
-        q8_ref[rows, :] = q4 * q4
+    @pl.when(jnp.logical_not(defers()))
+    def _():
+        tables(q_ref, r_ref, e_ref, q8_ref)
+
     for chunk in range(chunks):
         for copy in fetch(chunk):
             copy.wait()
@@ -165,7 +173,7 @@
     return before, run
 
 
-def ring_kernel(rate_ref, totals_ref, u_ref, r_ref, skip_ref, z_in_ref, wholes_ref, z_ref, q_ref, x_ref):
+def ring_kernel(rate_ref, totals_ref, u_ref, r_ref, skip_ref, z_in_ref, e_in_ref, q8_in_ref, wholes_ref, z_ref, e_ref, q8_ref, q_ref, x_ref):
     me = lax.axis_index("ctx")
     decay = decay_of(rate_ref[half_rates(rate_ref), :], float(CORES * LANES))
     before, run = prefix(lambda n: totals_ref[RING_ORDER.index(n)], RINGS, decay, me // CORES % RINGS)
@@ -176,6 +184,7 @@
     @pl.when(defers())
     def _():
         q_ref[...] = jnp.exp(-rate_ref[...])
+        tables(q_ref, r_ref, e_ref, q8_ref)
         recur(0, u_ref.shape[0] // (SUBS * SUBS), x_ref, u_ref, q_ref, r_ref, skip_ref, z_ref)
 
 
@@ -292,9 +301,10 @@
     ends = lax.all_gather(ends, "ctx", axis_index_groups=pairs)
     totals = call(chip_kernel, shape((RINGS, half, LANES), Z_TYPE), (), "chip")(rate_rows, ends)
     totals = swap(totals, along_z)
-    wholes, z = call(
-        ring_kernel, (shape((n_x * CORES, half, LANES), X_TYPE), table), (small, small), "ring", aliases={5: 1},
-    )(rate_rows, totals, u, residues, skip, z)
+    wholes, z, e, q8 = call(
+        ring_kernel, (shape((n_x * CORES, half, LANES), X_TYPE), table, weights, state), (small, small), "ring",
+        aliases={5: 1, 6: 2, 7: 3},
+    )(rate_rows, totals, u, residues, skip, z, e, q8)
     wholes = swap(wholes, along_x)
     gated, sums = call(
         gate_kernel,

time: 41.4 us -> 41.3 us (level)
  no operation moved by 1% of the time
where the time goes in v6:
time: 41.3 us; the launch traced here: 40.9 us
  blocking collectives  36.6 us (89%)
  Pallas kernels  4.31 us (10%)
    all_to_all x2, blocking collectives, swap(): lax.all_to_all(array, 'ctx', split_axis=0, concat_axis=0, tiled=True, axi...  18.8 us
    all_to_all x1, blocking collectives, per_device(): lax.all_to_all(sums, 'tp', split_axis=0, concat_axis=0, tiled=True, axis_...  9.34 us
    all_gather x1, blocking collectives, per_device(): ends = lax.all_gather(ends, 'ctx', axis_index_groups=pairs)  8.43 us
    pallas_call x1, Pallas kernels, per_device(): call(state_kernel, (state, table, weights, state, state, table, state, sh...  2.54 us
    pallas_call x1, Pallas kernels, per_device(): call(gate_kernel, (shape((tokens, width), bf16), shape((n_tp, tokens), f3...  0.86 us
    pallas_call x1, Pallas kernels, per_device(): call(functools.partial(norm_kernel, 1.0 / (n_tp * width)), shape((tokens,...  0.83 us

profile of v6, /device:TPU:1, one launch (start us, length us, event | category | flops | bytes accessed | tf_op | source)
XLA Modules:
  0.0 40.9 jit_solution(6593170258497092289)
XLA Ops:
  0.0 2.5 %states.1 = (f32[128,128]{1,0:T(8,128)S(1)}, f32[1024,128]{1,0:T(8,128)S(1)}, f32[1024,128]{1,0:T(8,128)S(1)}, f32[128,128]{1,0:T(8,128)S(1)}, f32[128,128]{1,0:...) custom-call(bf16[128,1024]{1,0:T(8,128)(2,1)} %k_hbm.1, ...), custom_call_target="tpu_custom_call" | custom-call | tf_op jit(solution)/shard_map/states/pallas_call | solution.py:292
  2.5 8.4 %all-gather = f32[256,128]{1,0:T(8,128)S(1)} all-gather(f32[128,128]{1,0:T(8,128)S(1)} %get-tuple-element.20), channel_id=2, replica_groups={{0,8},{16,24},{32,40},{48,56},{64,72},{80,88},{96,104},{112,120},{128,1..., dimensions={0}, use_global_device_ids=true | all-gather | bytes 196608 | tf_op jit(solution)/shard_map/all_gather | solution.py:301
  11.0 9.3 %all_to_all.21.totals_ref = bf16[8,64,128]{2,1,0:T(8,128)(2,1)S(1)} all-to-all(bf16[8,64,128]{2,1,0:T(8,128)(2,1)S(1)} %chip.1), channel_id=1, replica_groups={{96,112,0,16,32,48,64,80},{104,120,8,24,40,56,72,88},{224,240,128,144,1..., dimensions={0} | all-to-all | bytes 262144 | tf_op jit(solution)/shard_map/all_to_all | solution.py:285
  20.3 0.1 ring.1
  20.4 0.0 copy-start
  20.4 9.5 %all_to_all.22.wholes_ref = bf16[8,64,128]{2,1,0:T(8,128)(2,1)S(1)} all-to-all(bf16[8,64,128]{2,1,0:T(8,128)(2,1)S(1)} %get-tuple-element.30), channel_id=1, replica_groups={{264,0,8,128,136,256,384,392},{280,16,24,144,152,272,400,408},{296,32,4..., dimensions={0} | all-to-all | bytes 262144 | tf_op jit(solution)/shard_map/all_to_all | solution.py:285
  29.9 0.0 copy-done
  29.9 0.9 %gate.1 = (bf16[128,1024]{1,0:T(8,128)(2,1)S(1)}, f32[8,128]{1,0:T(8,128)S(1)}) custom-call(bf16[128,1024]{1,0:T(8,128)(2,1)S(1)} %copy-done, f32[1024,128]{1,0:T(8,128)S(1)} %get-tuple-element.27.z_ref, f32[1024,128]{1,0:T(8,128)S(1)} %get-tuple-element.28.e_ref, f32[128,128]{1,0:T(8,128)S(1)} %get-tuple-element.29.q8_ref, ...), custom_call_target="tpu_custom_call" | custom-call | tf_op jit(solution)/shard_map/gate/pallas_call | solution.py:309
  30.7 9.3 %all_to_all.23 = f32[8,1,128]{2,1,0:T(1,128)S(1)} all-to-all(f32[8,1,128]{2,1,0:T(1,128)S(1)} %bitcast.11), channel_id=1, replica_groups={{4,5,6,7,0,1,2,3},{12,13,14,15,8,9,10,11},{20,21,22,23,16,17,18,19},{28..., dimensions={0} | all-to-all | bytes 8192 | tf_op jit(solution)/shard_map/all_to_all | solution.py:314
  40.1 0.8 %norm.1 = bf16[128,1024]{1,0:T(8,128)(2,1)} custom-call(f32[8,128]{1,0:T(8,128)S(1)} %bitcast.10, bf16[128,1024]{1,0:T(8,128)(2,1)S(1)} %get-tuple-element.32.gated_ref), custom_call_target="tpu_custom_call" | custom-call | tf_op jit(solution)/shard_map/norm/pallas_call | solution.py:317
  (1 shorter events, 0.0 us)
Async XLA Ops:
  20.4 9.5 %copy-start = (bf16[128,1024]{1,0:T(8,128)(2,1)S(1)}, bf16[128,1024]{1,0:T(8,128)(2,1)}, u32[]{:S(2)}) copy-start(bf16[128,1024]{1,0:T(8,128)(2,1)} %q_ref.1) | copy-start | bytes 786436

commit v7 on v6

--- a/solution.py
+++ b/solution.py
@@ -78,18 +78,21 @@
         pltpu.make_async_copy(res_hbm, res_ref, mode_sems.at[1]),
         pltpu.make_async_copy(skip_hbm, skip_ref, mode_sems.at[2]),
     )
-    for copy in modes:
-        copy.start()
+    modes[0].start()
     for chunk in range(chunks):
         for copy in fetch(chunk):
             copy.start()
-    for copy in modes:
-        copy.wait()
+    for copy in modes[1:]:
+        copy.start()
+    modes[0].wait()
     fill_modes(rate_ref, rate_rows_ref, lambda r: r)
-    fill_modes(res_ref, r_ref, lambda r: r)
     q_ref[...] = jnp.exp(-rate_rows_ref[...])
+
     @pl.when(jnp.logical_not(defers()))
     def _():
+        for copy in modes[1:]:
+            copy.wait()
+        fill_modes(res_ref, r_ref, lambda r: r)
         tables(q_ref, r_ref, e_ref, q8_ref)
 
     for chunk in range(chunks):
@@ -112,6 +115,12 @@
         @pl.when(jnp.logical_not(defers()))
         def _():
             recur(*blocks, end_ref, u_ref, q_ref, r_ref, skip_ref, z_ref)
+
+    @pl.when(defers())
+    def _():
+        for copy in modes[1:]:
+            copy.wait()
+        fill_modes(res_ref, r_ref, lambda r: r)
 
 
 def defers():

time: 41.3 us -> 41.3 us (level)
  no operation moved by 1% of the time
where the time goes in v7:
time: 41.3 us; the launch traced here: 40.9 us
  blocking collectives  36.5 us (88%)
  Pallas kernels  4.36 us (11%)
    all_to_all x2, blocking collectives, swap(): lax.all_to_all(array, 'ctx', split_axis=0, concat_axis=0, tiled=True, axi...  18.7 us
    all_to_all x1, blocking collectives, per_device(): lax.all_to_all(sums, 'tp', split_axis=0, concat_axis=0, tiled=True, axis_...  9.34 us
    all_gather x1, blocking collectives, per_device(): ends = lax.all_gather(ends, 'ctx', axis_index_groups=pairs)  8.43 us
    pallas_call x1, Pallas kernels, per_device(): call(state_kernel, (state, table, weights, state, state, table, state, sh...  2.59 us
    pallas_call x1, Pallas kernels, per_device(): call(gate_kernel, (shape((tokens, width), bf16), shape((n_tp, tokens), f3...  0.86 us
    pallas_call x1, Pallas kernels, per_device(): call(functools.partial(norm_kernel, 1.0 / (n_tp * width)), shape((tokens,...  0.83 us

profile of v7, /device:TPU:1, one launch (start us, length us, event | category | flops | bytes accessed | tf_op | source)
XLA Modules:
  0.0 40.9 jit_solution(8586237321433042998)
XLA Ops:
  0.0 2.6 %states.1 = (f32[128,128]{1,0:T(8,128)S(1)}, f32[1024,128]{1,0:T(8,128)S(1)}, f32[1024,128]{1,0:T(8,128)S(1)}, f32[128,128]{1,0:T(8,128)S(1)}, f32[128,128]{1,0:...) custom-call(bf16[128,1024]{1,0:T(8,128)(2,1)} %k_hbm.1, ...), custom_call_target="tpu_custom_call" | custom-call | tf_op jit(solution)/shard_map/states/pallas_call | solution.py:301
  2.6 8.4 %all-gather = f32[256,128]{1,0:T(8,128)S(1)} all-gather(f32[128,128]{1,0:T(8,128)S(1)} %get-tuple-element.20), channel_id=2, replica_groups={{0,8},{16,24},{32,40},{48,56},{64,72},{80,88},{96,104},{112,120},{128,1..., dimensions={0}, use_global_device_ids=true | all-gather | bytes 196608 | tf_op jit(solution)/shard_map/all_gather | solution.py:310
  11.1 9.3 %all_to_all.21.totals_ref = bf16[8,64,128]{2,1,0:T(8,128)(2,1)S(1)} all-to-all(bf16[8,64,128]{2,1,0:T(8,128)(2,1)S(1)} %chip.1), channel_id=1, replica_groups={{96,112,0,16,32,48,64,80},{104,120,8,24,40,56,72,88},{224,240,128,144,1..., dimensions={0} | all-to-all | bytes 262144 | tf_op jit(solution)/shard_map/all_to_all | solution.py:294
  20.3 0.1 ring.1
  20.4 0.0 copy-start
  20.4 9.5 %all_to_all.22.wholes_ref = bf16[8,64,128]{2,1,0:T(8,128)(2,1)S(1)} all-to-all(bf16[8,64,128]{2,1,0:T(8,128)(2,1)S(1)} %get-tuple-element.30), channel_id=1, replica_groups={{264,0,8,128,136,256,384,392},{280,16,24,144,152,272,400,408},{296,32,4..., dimensions={0} | all-to-all | bytes 262144 | tf_op jit(solution)/shard_map/all_to_all | solution.py:294
  29.9 0.0 copy-done
  29.9 0.9 %gate.1 = (bf16[128,1024]{1,0:T(8,128)(2,1)S(1)}, f32[8,128]{1,0:T(8,128)S(1)}) custom-call(bf16[128,1024]{1,0:T(8,128)(2,1)S(1)} %copy-done, f32[1024,128]{1,0:T(8,128)S(1)} %get-tuple-element.27.z_ref, f32[1024,128]{1,0:T(8,128)S(1)} %get-tuple-element.28.e_ref, f32[128,128]{1,0:T(8,128)S(1)} %get-tuple-element.29.q8_ref, ...), custom_call_target="tpu_custom_call" | custom-call | tf_op jit(solution)/shard_map/gate/pallas_call | solution.py:318
  30.7 9.3 %all_to_all.23 = f32[8,1,128]{2,1,0:T(1,128)S(1)} all-to-all(f32[8,1,128]{2,1,0:T(1,128)S(1)} %bitcast.11), channel_id=1, replica_groups={{4,5,6,7,0,1,2,3},{12,13,14,15,8,9,10,11},{20,21,22,23,16,17,18,19},{28..., dimensions={0} | all-to-all | bytes 8192 | tf_op jit(solution)/shard_map/all_to_all | solution.py:323
  40.1 0.8 %norm.1 = bf16[128,1024]{1,0:T(8,128)(2,1)} custom-call(f32[8,128]{1,0:T(8,128)S(1)} %bitcast.10, bf16[128,1024]{1,0:T(8,128)(2,1)S(1)} %get-tuple-element.32.gated_ref), custom_call_target="tpu_custom_call" | custom-call | tf_op jit(solution)/shard_map/norm/pallas_call | solution.py:326
  (1 shorter events, 0.0 us)
Async XLA Ops:
  20.4 9.5 %copy-start = (bf16[128,1024]{1,0:T(8,128)(2,1)S(1)}, bf16[128,1024]{1,0:T(8,128)(2,1)}, u32[]{:S(2)}) copy-start(bf16[128,1024]{1,0:T(8,128)(2,1)} %q_ref.1) | copy-start | bytes 786436

commit v8 on v7

--- a/solution.py
+++ b/solution.py
@@ -15,7 +15,7 @@
 RING_ORDER = (6, 7, 0, 1, 2, 3, 4, 5)
 TP_ORDER = [4, 5, 6, 7, 0, 1, 2, 3]
 X_ORDER = ((2, 1), (0, 0), (0, 1), (1, 0), (1, 1), (2, 0), (3, 0), (3, 1))
-CHUNKS = 2
+CHUNKS = 1
 Z_TYPE = jnp.bfloat16
 X_TYPE = jnp.bfloat16
 

time: 41.3 us -> 41.4 us (level)
  no operation moved by 1% of the time
where the time goes in v8:
time: 41.4 us; the launch traced here: 41 us
  blocking collectives  36.7 us (89%)
  Pallas kernels  4.26 us (10%)
    all_to_all x2, blocking collectives, swap(): lax.all_to_all(array, 'ctx', split_axis=0, concat_axis=0, tiled=True, axi...  18.9 us
    all_to_all x1, blocking collectives, per_device(): lax.all_to_all(sums, 'tp', split_axis=0, concat_axis=0, tiled=True, axis_...  9.34 us
    all_gather x1, blocking collectives, per_device(): ends = lax.all_gather(ends, 'ctx', axis_index_groups=pairs)  8.43 us
    pallas_call x1, Pallas kernels, per_device(): call(state_kernel, (state, table, weights, state, state, table, state, sh...  2.49 us
    pallas_call x1, Pallas kernels, per_device(): call(gate_kernel, (shape((tokens, width), bf16), shape((n_tp, tokens), f3...  0.86 us
    pallas_call x1, Pallas kernels, per_device(): call(functools.partial(norm_kernel, 1.0 / (n_tp * width)), shape((tokens,...  0.83 us

profile of v8, /device:TPU:1, one launch (start us, length us, event | category | flops | bytes accessed | tf_op | source)
XLA Modules:
  0.0 41.0 jit_solution(3540174041246968208)
XLA Ops:
  0.0 2.5 %states.1 = (f32[128,128]{1,0:T(8,128)S(1)}, f32[1024,128]{1,0:T(8,128)S(1)}, f32[1024,128]{1,0:T(8,128)S(1)}, f32[128,128]{1,0:T(8,128)S(1)}, f32[128,128]{1,0:...) custom-call(bf16[128,1024]{1,0:T(8,128)(2,1)} %k_hbm.1, ...), custom_call_target="tpu_custom_call" | custom-call | tf_op jit(solution)/shard_map/states/pallas_call | solution.py:301
  2.5 8.4 %all-gather = f32[256,128]{1,0:T(8,128)S(1)} all-gather(f32[128,128]{1,0:T(8,128)S(1)} %get-tuple-element.20), channel_id=2, replica_groups={{0,8},{16,24},{32,40},{48,56},{64,72},{80,88},{96,104},{112,120},{128,1..., dimensions={0}, use_global_device_ids=true | all-gather | bytes 196608 | tf_op jit(solution)/shard_map/all_gather | solution.py:310
  11.0 9.4 %all_to_all.21.totals_ref = bf16[8,64,128]{2,1,0:T(8,128)(2,1)S(1)} all-to-all(bf16[8,64,128]{2,1,0:T(8,128)(2,1)S(1)} %chip.1), channel_id=1, replica_groups={{96,112,0,16,32,48,64,80},{104,120,8,24,40,56,72,88},{224,240,128,144,1..., dimensions={0} | all-to-all | bytes 262144 | tf_op jit(solution)/shard_map/all_to_all | solution.py:294
  20.4 0.1 ring.1
  20.5 0.0 copy-start
  20.5 9.5 %all_to_all.22.wholes_ref = bf16[8,64,128]{2,1,0:T(8,128)(2,1)S(1)} all-to-all(bf16[8,64,128]{2,1,0:T(8,128)(2,1)S(1)} %get-tuple-element.30), channel_id=1, replica_groups={{264,0,8,128,136,256,384,392},{280,16,24,144,152,272,400,408},{296,32,4..., dimensions={0} | all-to-all | bytes 262144 | tf_op jit(solution)/shard_map/all_to_all | solution.py:294
  29.9 0.0 copy-done
  29.9 0.9 %gate.1 = (bf16[128,1024]{1,0:T(8,128)(2,1)S(1)}, f32[8,128]{1,0:T(8,128)S(1)}) custom-call(bf16[128,1024]{1,0:T(8,128)(2,1)S(1)} %copy-done, f32[1024,128]{1,0:T(8,128)S(1)} %get-tuple-element.27.z_ref, f32[1024,128]{1,0:T(8,128)S(1)} %get-tuple-element.28.e_ref, f32[128,128]{1,0:T(8,128)S(1)} %get-tuple-element.29.q8_ref, ...), custom_call_target="tpu_custom_call" | custom-call | tf_op jit(solution)/shard_map/gate/pallas_call | solution.py:318
  30.8 9.3 %all_to_all.23 = f32[8,1,128]{2,1,0:T(1,128)S(1)} all-to-all(f32[8,1,128]{2,1,0:T(1,128)S(1)} %bitcast.11), channel_id=1, replica_groups={{4,5,6,7,0,1,2,3},{12,13,14,15,8,9,10,11},{20,21,22,23,16,17,18,19},{28..., dimensions={0} | all-to-all | bytes 8192 | tf_op jit(solution)/shard_map/all_to_all | solution.py:323
  40.1 0.8 %norm.1 = bf16[128,1024]{1,0:T(8,128)(2,1)} custom-call(f32[8,128]{1,0:T(8,128)S(1)} %bitcast.10, bf16[128,1024]{1,0:T(8,128)(2,1)S(1)} %get-tuple-element.32.gated_ref), custom_call_target="tpu_custom_call" | custom-call | tf_op jit(solution)/shard_map/norm/pallas_call | solution.py:326
  (1 shorter events, 0.0 us)
Async XLA Ops:
  20.5 9.5 %copy-start = (bf16[128,1024]{1,0:T(8,128)(2,1)S(1)}, bf16[128,1024]{1,0:T(8,128)(2,1)}, u32[]{:S(2)}) copy-start(bf16[128,1024]{1,0:T(8,128)(2,1)} %q_ref.1) | copy-start | bytes 786436
